TPU v7x, 32 devices: a whole 2x2x4 slice. The times are simulated.
32 devices in a mesh: facet: 8 (over y, x, core), slab: 4 (over z).
Axes of the slice: x: 2, y: 2, z: 4, core: 2. Of those that a mesh axis runs over, the one named last changes fastest.
Arguments:
- slab: bfloat16 [2, 8, 4096, 256], P(None, 'facet', 'slab'), may hold values from -6 to 6
- facet_offset: int32 [8], P('facet'), may hold values from 0 to 28672
- subgrid_offset: int32 [8], replicated, may hold values from 0 to 28672
- vis_cell: int32 [4, 8, 32768], P('slab', 'facet'), may hold values from 0 to 16383
- vis_value: float32 [2, 4, 8, 32768], P(None, 'slab', 'facet'), may hold values from -6 to 6
- vis_weight: float32 [4, 8, 32768], P('slab', 'facet'), may hold values from 0.1 to 1
Outputs:
- residual: float32 [2, 4, 512, 256], P(None, 'slab', 'facet')
- facet_update: float32 [2, 8, 4096, 256], P(None, 'facet', 'slab')
All inputs are finite; a program needn't handle non-finite values.
Results may differ from a plain program's by a relative error of at most 0.0041.
Values may be sent and summed in bfloat16 or wider, within the bound.
A program may use at most 64 MiB of HBM per device.

v0:
```python
import functools
import math

import jax
import jax.numpy as jnp
from jax import lax
from jax.experimental import pallas as pl
from jax.experimental.pallas import tpu as pltpu
from jax.sharding import PartitionSpec as P

IMAGE = 32768
SG = 256
UVSTEP = 16
F32 = jnp.float32
BF16 = jnp.bfloat16


def cis(turns):
    turns = turns & (IMAGE - 1)
    quarter = IMAGE // 4
    quad = (turns + quarter // 2) // quarter if quarter & (quarter - 1) else lax.shift_right_logical(
        turns + quarter // 2, quarter.bit_length() - 1
    )
    t = (turns - quad * quarter).astype(F32) * (2.0 * math.pi / IMAGE)
    z = t * t
    s = ((-1.9515295891e-4 * z + 8.3321608736e-3) * z - 1.6666654611e-1) * z * t + t
    c = ((2.443315711809948e-5 * z - 1.388731625493765e-3) * z + 4.166664568298827e-2) * z * z - 0.5 * z + 1.0
    odd = (quad & 1) == 1
    cos = jnp.where(odd, s, c)
    sin = jnp.where(odd, c, s)
    cos = jnp.where(((quad + 1) & 2) == 2, -cos, cos)
    sin = jnp.where((quad & 2) == 2, -sin, sin)
    return cos, sin


def grid_kernel(width, rows, cell_ref, value_ref, weight_ref, out_ref):
    @pl.when(pl.program_id(0) == 0)
    def _():
        out_ref[...] = jnp.zeros_like(out_ref)

    cell = cell_ref[...]
    weight = weight_ref[...]
    chunk = cell.shape[1]
    row = lax.shift_right_logical(cell, width.bit_length() - 1)
    col = cell & (width - 1)
    hot = jnp.where(lax.broadcasted_iota(jnp.int32, (width, chunk), 0) == col, 1.0, 0.0).astype(BF16)
    mine = lax.broadcasted_iota(jnp.int32, (rows, chunk), 0) == row
    terms = [weight * value_ref[0:1, :], weight * value_ref[1:2, :], weight]
    left = jnp.concatenate([jnp.where(mine, t, 0.0).astype(BF16) for t in terms], axis=0)
    out_ref[...] += lax.dot_general(left, hot, (((1,), (1,)), ((), ())), preferred_element_type=F32)


def grid_visibilities(cells, values, weights, owned, width):
    count = cells.shape[1]
    rows = -(-owned // 16) * 16
    chunk = min(count, 2048)
    out = pl.pallas_call(
        functools.partial(grid_kernel, width, rows),
        grid=(count // chunk,),
        in_specs=[
            pl.BlockSpec((1, chunk), lambda i: (0, i)),
            pl.BlockSpec((2, chunk), lambda i: (0, i)),
            pl.BlockSpec((1, chunk), lambda i: (0, i)),
        ],
        out_specs=pl.BlockSpec((3 * rows, width), lambda i: (0, 0)),
        out_shape=jax.ShapeDtypeStruct((3 * rows, width), F32),
        cost_estimate=pl.CostEstimate(flops=6 * rows * width * count, bytes_accessed=16 * count, transcendentals=0),
        name="gridding",
    )(cells, values, weights)
    return out.reshape(3, rows, width)[:, :owned]


def forward_kernel(first_ref, subs_ref, slab_ref, out_ref, cos_ref, sin_ref):
    s = pl.program_id(0)
    rows, local = cos_ref.shape
    first = first_ref[0]

    @pl.when(s == 0)
    def _():
        k = lax.broadcasted_iota(jnp.int32, (rows, local), 0)
        y = lax.broadcasted_iota(jnp.int32, (rows, local), 1) + first
        c, n = cis((UVSTEP * k) * y)
        cos_ref[...] = c
        sin_ref[...] = n

    y = lax.broadcasted_iota(jnp.int32, (8, local), 1) + first
    c1, s1 = cis(subs_ref[s] * y)
    c1, s1 = c1[0:1], s1[0:1]
    c2, s2 = cos_ref[...], sin_ref[...]
    tab_real = (c1 * c2 - s1 * s2).astype(BF16)
    tab_imag = (-(s1 * c2 + c1 * s2)).astype(BF16)
    re, im = slab_ref[0], slab_ref[1]
    dot = functools.partial(jnp.dot, preferred_element_type=F32)
    real = dot(tab_real, re) - dot(tab_imag, im)
    imag = dot(tab_real, im) + dot(tab_imag, re)
    slabs, band = out_ref.shape[1], out_ref.shape[3]
    for p in range(slabs):
        out_ref[0, p, 0] = real[p * band:(p + 1) * band].astype(out_ref.dtype)
        out_ref[1, p, 0] = imag[p * band:(p + 1) * band].astype(out_ref.dtype)


def forward(first, subs, slab, slabs):
    _, local, width = slab.shape
    count = subs.shape[0]
    band = SG // slabs
    return pl.pallas_call(
        forward_kernel,
        grid=(count,),
        in_specs=[
            pl.BlockSpec(memory_space=pltpu.SMEM),
            pl.BlockSpec(memory_space=pltpu.SMEM),
            pl.BlockSpec((2, local, width), lambda s: (0, 0, 0)),
        ],
        out_specs=pl.BlockSpec((2, slabs, 1, band, width), lambda s: (0, 0, s, 0, 0)),
        out_shape=jax.ShapeDtypeStruct((2, slabs, count, band, width), BF16),
        scratch_shapes=[pltpu.VMEM((SG, local), F32), pltpu.VMEM((SG, local), F32)],
        name="forward",
    )(first, subs, slab)


def adjoint_kernel(scale, slabs, first_ref, subs_ref, sent_ref, out_ref):
    tile = out_ref.shape[1]
    count = subs_ref.shape[1]
    band = SG // slabs
    start = first_ref[0] + pl.program_id(0) * tile
    yk = lax.broadcasted_iota(jnp.int32, (tile, SG), 0) + start
    c2, s2 = cis((UVSTEP * lax.broadcasted_iota(jnp.int32, (tile, SG), 1)) * yk)
    ys = lax.broadcasted_iota(jnp.int32, (tile, count), 0) + start
    c1, s1 = cis(ys * subs_ref[...])
    real = jnp.zeros(out_ref.shape[1:], F32)
    imag = jnp.zeros(out_ref.shape[1:], F32)
    dot = functools.partial(jnp.dot, preferred_element_type=F32)
    for s in range(count):
        a, b = c1[:, s:s + 1], s1[:, s:s + 1]
        tab_real = (a * c2 - b * s2).astype(BF16)
        tab_imag = (-(b * c2 + a * s2)).astype(BF16)
        re = jnp.concatenate([sent_ref[0, p, s] for p in range(slabs)], axis=0)
        im = jnp.concatenate([sent_ref[1, p, s] for p in range(slabs)], axis=0)
        real += dot(tab_real, re) + dot(tab_imag, im)
        imag += dot(tab_real, im) - dot(tab_imag, re)
    out_ref[0] = real * scale
    out_ref[1] = imag * scale


def adjoint(first, subs, sent, local):
    _, slabs, count, band, width = sent.shape
    tile = min(local, 256)
    return pl.pallas_call(
        functools.partial(adjoint_kernel, 1.0 / math.sqrt(count * SG), slabs),
        grid=(local // tile,),
        in_specs=[
            pl.BlockSpec(memory_space=pltpu.SMEM),
            pl.BlockSpec((1, count), lambda i: (0, 0)),
            pl.BlockSpec((2, slabs, count, band, width), lambda i: (0, 0, 0, 0, 0)),
        ],
        out_specs=pl.BlockSpec((2, tile, width), lambda i: (0, i, 0)),
        out_shape=jax.ShapeDtypeStruct((2, local, width), F32),
        name="adjoint",
    )(first, subs[None, :], sent)


def fused_kernel(
    scale, back, subs_ref, offset_ref, subv_ref, offv_ref, slab_ref, cell_ref, value_ref, weight_ref,
    residual_ref, update_ref,
    pslab, poff, cos_ref, sin_ref, acc, cb, rx, zf, zb, rz, sums, full, table,
    sw_send, sw_recv, x_send, x_recv, z_send, z_recv, gz_send, gz_recv, gx_send, gx_recv, gc_send, gc_recv,
):
    facets, slabs = lax.axis_size("facet"), lax.axis_size("slab")
    q, z = lax.axis_index("facet"), lax.axis_index("slab")
    core, chip = q % 2, q // 2
    chips = facets // 2
    partner = q + 1 - 2 * core
    _, local, width = slab_ref.shape
    band = SG // slabs
    dot = functools.partial(jnp.dot, preferred_element_type=F32)

    def at_chip(d):
        return 2 * ((chip + d) % chips) + core

    def from_chip(d):
        return 2 * ((chip + chips - d) % chips) + core

    def at_slab(e):
        return (z + e) % slabs

    def from_slab(e):
        return (z + slabs - e) % slabs

    def remote(src, dst, send, recv, **where):
        return pltpu.make_async_remote_copy(
            src_ref=src, dst_ref=dst, send_sem=send, recv_sem=recv,
            device_id=where, device_id_type=pl.DeviceIdType.MESH,
        )

    barrier = pltpu.get_barrier_semaphore()
    pl.semaphore_signal(barrier, inc=1, device_id={"facet": partner}, device_id_type=pl.DeviceIdType.MESH)
    for d in range(1, chips):
        pl.semaphore_signal(barrier, inc=1, device_id={"facet": at_chip(d)}, device_id_type=pl.DeviceIdType.MESH)
    for e in range(1, slabs):
        pl.semaphore_signal(barrier, inc=1, device_id={"slab": at_slab(e)}, device_id_type=pl.DeviceIdType.MESH)
    pl.semaphore_wait(barrier, chips + slabs - 1)

    swap_offset = remote(offv_ref, poff, sw_send.at[0], sw_recv.at[0], facet=partner)
    swap_slab = remote(slab_ref, pslab, sw_send.at[1], sw_recv.at[1], facet=partner)
    swap_offset.start()
    swap_slab.start()

    first = offset_ref[0] + z * local

    def build(y, slot):
        def step(i, carry):
            k = lax.broadcasted_iota(jnp.int32, (32, local), 0) + i * 32
            c, n = cis((UVSTEP * k) * y[0:1, :])
            at = pl.ds(pl.multiple_of(i * 32, 32), 32)
            cos_ref[slot, at] = c
            sin_ref[slot, at] = n
            return carry

        lax.fori_loop(0, SG // 32, step, 0)

    def partial_sum(s, y, slot, data_ref):
        c1, s1 = cis(subs_ref[s] * y)
        c1, s1 = c1[0:1], s1[0:1]
        c2, s2 = cos_ref[slot], sin_ref[slot]
        tab_real = (c1 * c2 - s1 * s2).astype(BF16)
        tab_imag = (-(s1 * c2 + c1 * s2)).astype(BF16)
        re, im = data_ref[0], data_ref[1]
        return dot(tab_real, re) - dot(tab_imag, im), dot(tab_real, im) + dot(tab_imag, re)

    line = lax.broadcasted_iota(jnp.int32, (8, local), 1)
    places = line + first
    build(places, 0)

    def own_part(d, carry):
        real, imag = partial_sum(at_chip(d), places, 0, slab_ref)
        acc[d, 0] = real
        acc[d, 1] = imag
        return carry

    lax.fori_loop(0, chips, own_part, 0)
    swap_offset.wait()
    pplaces = line + (poff[:, 0:1] + z * local)
    build(pplaces, 1)
    swap_slab.wait()
    x_copies = []
    for d in list(range(1, chips)) + [0]:
        real, imag = partial_sum(at_chip(d), pplaces, 1, pslab)
        if d == 0:
            acc[0, 0] += real
            acc[0, 1] += imag
        else:
            cb[d - 1, 0] = (acc[d, 0] + real).astype(BF16)
            cb[d - 1, 1] = (acc[d, 1] + imag).astype(BF16)
            copy = remote(cb.at[d - 1], rx.at[d - 1], x_send.at[d - 1], x_recv.at[d - 1], facet=at_chip(d))
            copy.start()
            x_copies.append(copy)

    rows = sums.shape[0] // 3
    count = cell_ref.shape[1]
    chunk = min(count, 2048)
    sums[...] = jnp.zeros_like(sums)

    def grid_step(i, carry):
        at = pl.ds(pl.multiple_of(i * chunk, chunk), chunk)
        cell = cell_ref[:, at]
        weight = weight_ref[:, at]
        row = lax.shift_right_logical(cell, width.bit_length() - 1).astype(F32)
        col = (cell & (width - 1)).astype(F32)
        lines = lax.broadcasted_iota(jnp.int32, (16, chunk), 0).astype(F32).astype(BF16)
        row = jnp.broadcast_to(row, (16, chunk)).astype(BF16)
        col = jnp.broadcast_to(col, (16, chunk)).astype(BF16)
        one, zero = jnp.ones((16, chunk), BF16), jnp.zeros((16, chunk), BF16)
        hot = jnp.concatenate(
            [jnp.where(col == lines + jnp.asarray(g, BF16), one, zero) for g in range(0, width, 16)], axis=0
        )
        terms = [weight * value_ref[0, :, at], weight * value_ref[1, :, at], weight]
        terms = [jnp.broadcast_to(t, (16, chunk)).astype(BF16) for t in terms]
        left = jnp.concatenate(
            [jnp.where(row == lines + jnp.asarray(g, BF16), t, zero) for t in terms for g in range(0, rows, 16)],
            axis=0,
        )
        sums[...] += lax.dot_general(left, hot, (((1,), (1,)), ((), ())), preferred_element_type=F32)
        return carry

    chunks = count // chunk
    early = (5 * chunks) // 8
    lax.fori_loop(0, early, grid_step, 0)

    for copy in x_copies:
        copy.wait()
    for p in range(slabs):
        for c in range(2):
            at = slice(p * band, (p + 1) * band)
            total = acc[0, c, at]
            for d in range(1, chips):
                total += rx[d - 1, c, at].astype(F32)
            zf[p, c] = total
            zb[p, c] = total.astype(BF16)
    z_copies = []
    for e in range(1, slabs):
        copy = remote(zb.at[at_slab(e)], rz.at[e - 1], z_send.at[e - 1], z_recv.at[e - 1], slab=at_slab(e))
        copy.start()
        z_copies.append(copy)

    tile = min(local, 256)

    lax.fori_loop(early, chunks, grid_step, 0)

    for copy in z_copies:
        copy.wait()
    for c in range(2):
        model = zf[z, c]
        for e in range(1, slabs):
            model += rz[e - 1, c].astype(F32)
        piece = sums[c * rows:c * rows + band] - sums[2 * rows:2 * rows + band] * (model * scale)
        residual_ref[c] = piece
        full[q, z, c] = piece.astype(BF16)

    def table_step(i, carry):
        at = pl.ds(pl.multiple_of(i * tile, tile), tile)
        y = lax.broadcasted_iota(jnp.int32, (tile, 1), 0) + (first + i * tile)
        c2, s2 = cis((UVSTEP * lax.broadcasted_iota(jnp.int32, (tile, SG), 1)) * y)
        c1, s1 = cis(y * subv_ref[...])
        for s in range(facets):
            a, b = c1[:, s:s + 1], s1[:, s:s + 1]
            table[s, 0, at] = (a * c2 - b * s2).astype(BF16)
            table[s, 1, at] = (-(b * c2 + a * s2)).astype(BF16)
        return carry

    late = []

    def spread(s, p, e, d):
        ref = full.at[s, p]
        copy = remote(ref, ref, gc_send.at[e, d], gc_recv.at[e, d], facet=partner)
        copy.start()
        late.append(copy)

    def across(p, e):
        ref = full.at[q, p]
        out = []
        for d in range(1, chips):
            copy = remote(ref, ref, gx_send.at[e, d - 1], gx_recv.at[e, d - 1], facet=at_chip(d))
            copy.start()
            out.append(copy)
        return out

    own = full.at[q, z]
    g_copies = []
    for e in range(1, slabs):
        copy = remote(own, own, gz_send.at[e - 1], gz_recv.at[e - 1], slab=at_slab(e))
        copy.start()
        g_copies.append(copy)
    a_copies = [across(z, 0)]
    spread(q, z, 0, 0)
    tiles = local // tile
    done = 0
    for e in range(1, slabs):
        share = (e * tiles) // slabs
        lax.fori_loop(done, share, table_step, 0)
        done = share
        g_copies[e - 1].wait_recv()
        a_copies.append(across(from_slab(e), e))
        spread(q, from_slab(e), e, 0)
    lax.fori_loop(done, tiles, table_step, 0)

    def update_pass(which, begin, end):
        def step(i, carry):
            at = pl.ds(pl.multiple_of(i * tile, tile), tile)
            real = imag = None
            for s in which:
                tab_real, tab_imag = table[s, 0, at], table[s, 1, at]
                re = jnp.concatenate([full[s, p, 0] for p in range(slabs)], axis=0)
                im = jnp.concatenate([full[s, p, 1] for p in range(slabs)], axis=0)
                dr = dot(tab_real, re) + dot(tab_imag, im)
                di = dot(tab_real, im) - dot(tab_imag, re)
                real = dr if real is None else real + dr
                imag = di if imag is None else imag + di
            if not begin:
                real += update_ref[0, at]
                imag += update_ref[1, at]
            update_ref[0, at] = real * back if end else real
            update_ref[1, at] = imag * back if end else imag
            return carry

        lax.fori_loop(0, tiles, step, 0)

    def relay(e):
        for d in range(1, chips):
            a_copies[e][d - 1].wait_recv()
            spread(from_chip(d), from_slab(e), e, d)

    relay(0)
    update_pass([q], True, False)
    for e in range(1, slabs - 1):
        relay(e)
    for copy in late[:slabs]:
        copy.wait_recv()
    update_pass([partner], False, False)
    relay(slabs - 1)
    update_pass([from_chip(d) for d in range(1, chips)], False, False)
    for copy in late[slabs:]:
        copy.wait_recv()
    update_pass([from_chip(d) + 1 - 2 * core for d in range(1, chips)], False, True)
    for copy in g_copies + late:
        copy.wait_send()
    for group in a_copies:
        for copy in group:
            copy.wait_send()


def fused(offset, subs, slab, cells, values, weights, slabs, facets):
    _, local, width = slab.shape
    band = SG // slabs
    chips = facets // 2
    rows = -(-band // 16) * 16
    vmem = pl.BlockSpec(memory_space=pltpu.VMEM)
    dma = pltpu.SemaphoreType.DMA
    return pl.pallas_call(
        functools.partial(
            fused_kernel, 1.0 / math.sqrt(local * slabs * facets), 1.0 / math.sqrt(subs.shape[0] * SG)
        ),
        in_specs=[pl.BlockSpec(memory_space=pltpu.SMEM)] * 2 + [vmem] * 6,
        out_specs=[vmem, vmem],
        out_shape=[
            jax.ShapeDtypeStruct((2, band, width), F32),
            jax.ShapeDtypeStruct((2, local, width), F32),
        ],
        scratch_shapes=[
            pltpu.VMEM((2, local, width), BF16),
            pltpu.VMEM((8, 128), jnp.int32),
            pltpu.VMEM((2, SG, local), F32),
            pltpu.VMEM((2, SG, local), F32),
            pltpu.VMEM((chips, 2, SG, width), F32),
            pltpu.VMEM((chips - 1, 2, SG, width), BF16),
            pltpu.VMEM((chips - 1, 2, SG, width), BF16),
            pltpu.VMEM((slabs, 2, band, width), F32),
            pltpu.VMEM((slabs, 2, band, width), BF16),
            pltpu.VMEM((slabs - 1, 2, band, width), BF16),
            pltpu.VMEM((3 * rows, width), F32),
            pltpu.VMEM((facets, slabs, 2, band, width), BF16),
            pltpu.VMEM((facets, 2, local, SG), BF16),
            dma((2,)), dma((2,)),
            dma((chips - 1,)), dma((chips - 1,)),
            dma((slabs - 1,)), dma((slabs - 1,)),
            dma((slabs - 1,)), dma((slabs - 1,)),
            dma((slabs, chips - 1)), dma((slabs, chips - 1)),
            dma((slabs, chips)), dma((slabs, chips)),
        ],
        compiler_params=pltpu.CompilerParams(collective_id=0, has_side_effects=True, vmem_limit_bytes=36 * 1024 * 1024),
        name="fused",
    )(subs, offset, subs[None, :], jnp.broadcast_to(offset, (8, 128)), slab, cells, values, weights)


def body(slab, facet_offset, subgrid_offset, vis_cell, vis_value, vis_weight):
    slabs = lax.axis_size("slab")
    facets = lax.axis_size("facet")
    local_rows = slab.shape[2]
    width = slab.shape[3]
    count_sub = subgrid_offset.shape[0]
    band = SG // slabs
    owned = count_sub * band // facets
    first = (facet_offset + lax.axis_index("slab") * local_rows).astype(jnp.int32)
    if owned == band and facets % 2 == 0 and facets > 2 and slabs > 1 and band % 16 == 0:
        residual, update = fused(
            facet_offset, subgrid_offset, slab[:, 0], vis_cell[0], vis_value[:, 0], vis_weight[0], slabs, facets
        )
        return (residual.reshape(2, 1, owned, width), update.reshape(2, 1, local_rows, width))
    sums = grid_visibilities(vis_cell[0], vis_value[:, 0, 0], vis_weight[0], owned, width)
    contrib = forward(first, subgrid_offset, slab[:, 0], slabs)
    contrib = contrib.reshape(2, slabs, facets, owned, width)
    parts = lax.all_to_all(contrib, "facet", 2, 2, tiled=True)
    parts = jnp.sum(parts, axis=2, dtype=F32).astype(BF16)
    parts = lax.all_to_all(parts, "slab", 1, 1, tiled=True)
    scale = 1.0 / math.sqrt(local_rows * slabs * facets)
    model = jnp.sum(parts, axis=1, dtype=F32) * scale
    residual = sums[:2] - sums[2:] * model
    sent = residual.astype(BF16).reshape(2, 1, 1, owned, width)
    piece = lax.all_gather(sent, "slab", axis=1, tiled=True)
    piece = lax.all_gather(piece, "facet", axis=2, tiled=True)
    piece = piece.reshape(2, slabs, count_sub, band, width)
    update = adjoint(first, subgrid_offset, piece, local_rows)
    return (residual.reshape(2, 1, owned, width), update.reshape(2, 1, local_rows, width))


def solution(mesh):
    placed = (
        P(None, "facet", "slab", None),
        P("facet"),
        P(),
        P("slab", "facet", None),
        P(None, "slab", "facet", None),
        P("slab", "facet", None),
    )
    return jax.shard_map(
        body,
        mesh=mesh,
        in_specs=placed,
        out_specs=(P(None, "slab", "facet", None), P(None, "facet", "slab", None)),
        check_vma=False,
    )
```

profile of v0, /device:TPU:0, one launch (start us, length us, event | category | flops | bytes accessed | tf_op | source)
XLA Modules:
  0.0 58.6 jit_solution(11413973841380541350)
XLA Ops:
  1.3 0.0 copy-start
  1.3 1.2 %copy-done = bf16[2,1,1024,256]{3,2,1,0:T(8,128)(2,1)S(1)} copy-done((bf16[2,1,1024,256]{3,2,1,0:T(8,128)(2,1)S(1)}, bf16[2,1,1024,256]{3,2,1,0:T(8,128)(2,1)}, u32[]{:S(2)}) %copy-start) | copy-done | bytes 1048600
  2.5 0.0 copy-start.1
  2.5 0.9 %copy-done.1 = f32[2,1,1,32768]{3,2,1,0:T(1,128)S(1)} copy-done((f32[2,1,1,32768]{3,2,1,0:T(1,128)S(1)}, f32[2,1,1,32768]{3,2,1,0:T(1,128)}, u32[]{:S(2)}) %copy-start.1) | copy-done | bytes 262168
  3.5 0.0 copy-start.2
  3.5 0.9 %copy-done.2 = s32[1,1,32768]{2,1,0:T(1,128)S(1)} copy-done((s32[1,1,32768]{2,1,0:T(1,128)S(1)}, s32[1,1,32768]{2,1,0:T(1,128)}, u32[]{:S(2)}) %copy-start.2) | copy-done | bytes 131096
  4.4 0.0 copy-start.3
  4.4 0.9 %copy-done.3 = f32[1,1,32768]{2,1,0:T(1,128)S(1)} copy-done((f32[1,1,32768]{2,1,0:T(1,128)S(1)}, f32[1,1,32768]{2,1,0:T(1,128)}, u32[]{:S(2)}) %copy-start.3) | copy-done | bytes 131096
  5.3 0.0 copy-start.4
  5.3 0.7 %copy-done.4 = s32[8]{0:T(128)S(1)} copy-done((s32[8]{0:T(128)S(1)}, s32[8]{0:T(128)}, u32[]{:S(2)}) %copy-start.4) | copy-done | bytes 56
  5.9 50.6 %fused.1 = (f32[2,64,256]{2,1,0:T(8,128)S(1)}, f32[2,1024,256]{2,1,0:T(8,128)S(1)}) custom-call(s32[8]{0:T(128)S(1)} %copy-done.4, s32[1]{0:T(128)} %copy.12.offset_ref, s32[1,8]{1,0:T(1,128)S(1)} %bitcast.19, s32[8,128]{1,0:T(8,128)S(1)} %broadcast_in_dim.9.offv_ref, bf16[2,1024,256]{2,1,0:T(8,128)(2,1)S(1)} %bitcast.14, s32[1,32768]{1,0:T(1,128)S(1)} %bitcast.16, ...), custom_call_target="tpu_custom_call" | custom-call | tf_op jit(solution)/shard_map/fused/pallas_call | solution.py:418
  56.6 0.7 %copy.13 = f32[2,1,64,256]{3,2,1,0:T(8,128)} copy(f32[2,1,64,256]{3,2,1,0:T(8,128)S(1)} %bitcast.18) | data formatting | bytes 262144
  57.2 1.3 %copy.14 = f32[2,1,1024,256]{3,2,1,0:T(8,128)} copy(f32[2,1,1024,256]{3,2,1,0:T(8,128)S(1)} %bitcast.13) | data formatting | bytes 4194304
  (1 shorter events, 0.0 us)
Async XLA Ops:
  1.3 1.2 %copy-start = (bf16[2,1,1024,256]{3,2,1,0:T(8,128)(2,1)S(1)}, bf16[2,1,1024,256]{3,2,1,0:T(8,128)(2,1)}, u32[]{:S(2)}) copy-start(bf16[2,1,1024,256]{3,2,1,0:T(8,128)(2,1)} %param.6) | copy-start | bytes 3145732
  2.5 0.9 %copy-start.1 = (f32[2,1,1,32768]{3,2,1,0:T(1,128)S(1)}, f32[2,1,1,32768]{3,2,1,0:T(1,128)}, u32[]{:S(2)}) copy-start(f32[2,1,1,32768]{3,2,1,0:T(1,128)} %param.10) | copy-start | bytes 786436
  3.5 0.9 %copy-start.2 = (s32[1,1,32768]{2,1,0:T(1,128)S(1)}, s32[1,1,32768]{2,1,0:T(1,128)}, u32[]{:S(2)}) copy-start(s32[1,1,32768]{2,1,0:T(1,128)} %param.9) | copy-start | bytes 393220
  4.4 0.9 %copy-start.3 = (f32[1,1,32768]{2,1,0:T(1,128)S(1)}, f32[1,1,32768]{2,1,0:T(1,128)}, u32[]{:S(2)}) copy-start(f32[1,1,32768]{2,1,0:T(1,128)} %param.11) | copy-start | bytes 393220
  5.3 0.7 %copy-start.4 = (s32[8]{0:T(128)S(1)}, s32[8]{0:T(128)}, u32[]{:S(2)}) copy-start(s32[8]{0:T(128)} %subs_ref.1) | copy-start | bytes 100
where the time goes:
time: 59.6 us; the launch traced here: 58.6 us
  Pallas kernels  50.6 us (85%)
  local copies, waits for them, and re-layouts  6.61 us (11%)
  between operations  1.31 us (2%)
    pallas_call x1, Pallas kernels, fused(): pl.pallas_call(functools.partial(fused_kernel, 1.0 / math.sqrt(local * sl...  50.6 us
    unnamed x12, local copies, waits for them, and re-layouts  6.61 us

commit v1 on v0

--- a/solution.py
+++ b/solution.py
@@ -160,9 +160,10 @@
 
 
 def fused_kernel(
-    scale, back, subs_ref, offset_ref, subv_ref, offv_ref, slab_ref, cell_ref, value_ref, weight_ref,
+    scale, back, subs_ref, offset_ref, offv_ref, slab_hbm, cell_hbm, value_hbm, weight_hbm,
     residual_ref, update_ref,
-    pslab, poff, cos_ref, sin_ref, acc, cb, rx, zf, zb, rz, sums, full, table,
+    slab_ref, pslab, cell_ref, value_ref, weight_ref, poff, low, high, acc, cb, rx, zf, zb, rz, sums, full,
+    table, turn, load,
     sw_send, sw_recv, x_send, x_recv, z_send, z_recv, gz_send, gz_recv, gx_send, gx_recv, gc_send, gc_recv,
 ):
     facets, slabs = lax.axis_size("facet"), lax.axis_size("slab")
@@ -172,19 +173,11 @@
     partner = q + 1 - 2 * core
     _, local, width = slab_ref.shape
     band = SG // slabs
+    groups = band // 16
     dot = functools.partial(jnp.dot, preferred_element_type=F32)
 
     def at_chip(d):
-        return 2 * ((chip + d) % chips) + core
-
-    def from_chip(d):
-        return 2 * ((chip + chips - d) % chips) + core
-
-    def at_slab(e):
-        return (z + e) % slabs
-
-    def from_slab(e):
-        return (z + slabs - e) % slabs
+        return 2 * (chip ^ d) + core
 
     def remote(src, dst, send, recv, **where):
         return pltpu.make_async_remote_copy(
@@ -193,71 +186,93 @@
         )
 
     barrier = pltpu.get_barrier_semaphore()
-    pl.semaphore_signal(barrier, inc=1, device_id={"facet": partner}, device_id_type=pl.DeviceIdType.MESH)
+    for e in range(1, slabs):
+        pl.semaphore_signal(barrier, inc=1, device_id={"slab": z ^ e}, device_id_type=pl.DeviceIdType.MESH)
     for d in range(1, chips):
         pl.semaphore_signal(barrier, inc=1, device_id={"facet": at_chip(d)}, device_id_type=pl.DeviceIdType.MESH)
-    for e in range(1, slabs):
-        pl.semaphore_signal(barrier, inc=1, device_id={"slab": at_slab(e)}, device_id_type=pl.DeviceIdType.MESH)
+    pl.semaphore_signal(barrier, inc=1, device_id={"facet": partner}, device_id_type=pl.DeviceIdType.MESH)
+    loads = [
+        pltpu.make_async_copy(src, dst, load.at[i])
+        for i, (src, dst) in enumerate(
+            [(slab_hbm, slab_ref), (cell_hbm, cell_ref), (value_hbm, value_ref), (weight_hbm, weight_ref)]
+        )
+    ]
+    for copy in loads:
+        copy.start()
+
+    first = offset_ref[0] + z * local
+    line = lax.broadcasted_iota(jnp.int32, (16, local), 1)
+
+    def build_low(places, slot):
+        c, n = cis(UVSTEP * lax.broadcasted_iota(jnp.int32, (16, local), 0) * places)
+        low[slot, 0] = c
+        low[slot, 1] = n
+
+    def partial_sum(p, places, slot, data_ref):
+        row = lax.broadcasted_iota(jnp.int32, (chips * groups, local), 0)
+        freq = UVSTEP * (band * p + 16 * (row % groups))
+        for d in range(chips):
+            freq += jnp.where(row // groups == d, subs_ref[at_chip(d)], 0)
+        c, n = cis(freq * places[0:1])
+        high[0] = c
+        high[1] = n
+        c2, s2 = low[slot, 0], low[slot, 1]
+        cos, sin = [], []
+        for g in range(chips * groups):
+            c1, s1 = high[0, g:g + 1], high[1, g:g + 1]
+            cos.append((c1 * c2 - s1 * s2).astype(BF16))
+            sin.append((s1 * c2 + c1 * s2).astype(BF16))
+        cos = jnp.concatenate(cos, axis=0)
+        sin = jnp.concatenate(sin, axis=0)
+        data = data_ref[...].reshape(2 * local, width)
+        real = dot(jnp.concatenate([cos, sin], axis=1), data)
+        imag = dot(jnp.concatenate([-sin, cos], axis=1), data)
+        return real, imag
+
+    places = line + first
+    build_low(places, 0)
+    loads[0].wait()
     pl.semaphore_wait(barrier, chips + slabs - 1)
-
     swap_offset = remote(offv_ref, poff, sw_send.at[0], sw_recv.at[0], facet=partner)
     swap_slab = remote(slab_ref, pslab, sw_send.at[1], sw_recv.at[1], facet=partner)
     swap_offset.start()
     swap_slab.start()
 
-    first = offset_ref[0] + z * local
-
-    def build(y, slot):
-        def step(i, carry):
-            k = lax.broadcasted_iota(jnp.int32, (32, local), 0) + i * 32
-            c, n = cis((UVSTEP * k) * y[0:1, :])
-            at = pl.ds(pl.multiple_of(i * 32, 32), 32)
-            cos_ref[slot, at] = c
-            sin_ref[slot, at] = n
-            return carry
-
-        lax.fori_loop(0, SG // 32, step, 0)
-
-    def partial_sum(s, y, slot, data_ref):
-        c1, s1 = cis(subs_ref[s] * y)
-        c1, s1 = c1[0:1], s1[0:1]
-        c2, s2 = cos_ref[slot], sin_ref[slot]
-        tab_real = (c1 * c2 - s1 * s2).astype(BF16)
-        tab_imag = (-(s1 * c2 + c1 * s2)).astype(BF16)
-        re, im = data_ref[0], data_ref[1]
-        return dot(tab_real, re) - dot(tab_imag, im), dot(tab_real, im) + dot(tab_imag, re)
-
-    line = lax.broadcasted_iota(jnp.int32, (8, local), 1)
-    places = line + first
-    build(places, 0)
-
-    def own_part(d, carry):
-        real, imag = partial_sum(at_chip(d), places, 0, slab_ref)
-        acc[d, 0] = real
-        acc[d, 1] = imag
+    def own_part(i, carry):
+        real, imag = partial_sum(z ^ (slabs - 1 - i), places, 0, slab_ref)
+        acc[i, 0] = real
+        acc[i, 1] = imag
         return carry
 
-    lax.fori_loop(0, chips, own_part, 0)
+    lax.fori_loop(0, slabs, own_part, 0)
     swap_offset.wait()
-    pplaces = line + (poff[:, 0:1] + z * local)
-    build(pplaces, 1)
+    pplaces = line + (poff[0:1, 0:1] + z * local)
+    build_low(pplaces, 1)
     swap_slab.wait()
-    x_copies = []
-    for d in list(range(1, chips)) + [0]:
-        real, imag = partial_sum(at_chip(d), pplaces, 1, pslab)
-        if d == 0:
-            acc[0, 0] += real
-            acc[0, 1] += imag
-        else:
-            cb[d - 1, 0] = (acc[d, 0] + real).astype(BF16)
-            cb[d - 1, 1] = (acc[d, 1] + imag).astype(BF16)
-            copy = remote(cb.at[d - 1], rx.at[d - 1], x_send.at[d - 1], x_recv.at[d - 1], facet=at_chip(d))
-            copy.start()
-            x_copies.append(copy)
+
+    def x_copy(i, d):
+        return remote(
+            cb.at[i, d - 1], rx.at[i, d - 1], x_send.at[i, d - 1], x_recv.at[i, d - 1], facet=at_chip(d)
+        )
+
+    def partner_part(i, carry):
+        real, imag = partial_sum(z ^ (slabs - 1 - i), pplaces, 1, pslab)
+        for c, part in enumerate((real, imag)):
+            for d in range(1, chips):
+                at = slice(d * band, (d + 1) * band)
+                cb[i, d - 1, c] = (acc[i, c, at] + part[at]).astype(BF16)
+            zf[i, c] = acc[i, c, 0:band] + part[0:band]
+        for d in range(chips - 1, 0, -1):
+            x_copy(i, d).start()
+        return carry
+
+    lax.fori_loop(0, slabs, partner_part, 0)
 
     rows = sums.shape[0] // 3
     count = cell_ref.shape[1]
     chunk = min(count, 2048)
+    for copy in loads[1:]:
+        copy.wait()
     sums[...] = jnp.zeros_like(sums)
 
     def grid_step(i, carry):
@@ -282,99 +297,97 @@
         sums[...] += lax.dot_general(left, hot, (((1,), (1,)), ((), ())), preferred_element_type=F32)
         return carry
 
+    span = facets * band
+
+    def table_band(p, carry):
+        lane = lax.broadcasted_iota(jnp.int32, (16, span), 1)
+        freq = UVSTEP * (band * p + lane % band)
+        for s in range(facets):
+            freq += jnp.where(lane // band == s, subs_ref[s], 0)
+        c2, s2 = cis(freq * lax.broadcasted_iota(jnp.int32, (16, span), 0))
+        far = first + 16 * lax.broadcasted_iota(jnp.int32, (local // 16, span), 0)
+        c, n = cis(freq[0:1] * far)
+        turn[0] = c
+        turn[1] = n
+
+        def step(g, inner):
+            c1, s1 = turn[0, pl.ds(g, 1)], turn[1, pl.ds(g, 1)]
+            sin = (s1 * c2 + c1 * s2).astype(BF16)
+            at = pl.ds(pl.multiple_of(g * 16, 16), 16)
+            table[p, at, 0:span] = sin
+            table[p, at, span:2 * span] = (c1 * c2 - s1 * s2).astype(BF16)
+            table[p, at, 2 * span:3 * span] = -sin
+            return inner
+
+        lax.fori_loop(0, local // 16, step, 0)
+        return carry
+
     chunks = count // chunk
-    early = (5 * chunks) // 8
-    lax.fori_loop(0, early, grid_step, 0)
-
-    for copy in x_copies:
-        copy.wait()
-    for p in range(slabs):
+    cuts = [0, (6 * chunks) // 16, (9 * chunks) // 16, (13 * chunks) // 16, chunks]
+    cuts = [cuts[min(i, 4)] for i in range(slabs)] + [chunks]
+
+    def z_copy(i):
+        return remote(zb.at[i], rz.at[i], z_send.at[i], z_recv.at[i], slab=z ^ (slabs - 1 - i))
+
+    model = []
+    for i in range(slabs):
+        lax.fori_loop(cuts[i], cuts[i + 1], grid_step, 0)
+        for d in range(chips - 1, 0, -1):
+            x_copy(i, d).wait()
         for c in range(2):
-            at = slice(p * band, (p + 1) * band)
-            total = acc[0, c, at]
+            total = zf[i, c]
             for d in range(1, chips):
-                total += rx[d - 1, c, at].astype(F32)
-            zf[p, c] = total
-            zb[p, c] = total.astype(BF16)
-    z_copies = []
-    for e in range(1, slabs):
-        copy = remote(zb.at[at_slab(e)], rz.at[e - 1], z_send.at[e - 1], z_recv.at[e - 1], slab=at_slab(e))
-        copy.start()
-        z_copies.append(copy)
-
-    tile = min(local, 256)
-
-    lax.fori_loop(early, chunks, grid_step, 0)
-
-    for copy in z_copies:
-        copy.wait()
+                total += rx[i, d - 1, c].astype(F32)
+            if i < slabs - 1:
+                zb[i, c] = total.astype(BF16)
+            else:
+                zf[i, c] = total
+        if i < slabs - 1:
+            z_copy(i).start()
+    for i in range(slabs - 1):
+        z_copy(i).wait()
     for c in range(2):
-        model = zf[z, c]
-        for e in range(1, slabs):
-            model += rz[e - 1, c].astype(F32)
+        model = zf[slabs - 1, c]
+        for i in range(slabs - 1):
+            model += rz[i, c].astype(F32)
         piece = sums[c * rows:c * rows + band] - sums[2 * rows:2 * rows + band] * (model * scale)
         residual_ref[c] = piece
-        full[q, z, c] = piece.astype(BF16)
-
-    def table_step(i, carry):
-        at = pl.ds(pl.multiple_of(i * tile, tile), tile)
-        y = lax.broadcasted_iota(jnp.int32, (tile, 1), 0) + (first + i * tile)
-        c2, s2 = cis((UVSTEP * lax.broadcasted_iota(jnp.int32, (tile, SG), 1)) * y)
-        c1, s1 = cis(y * subv_ref[...])
-        for s in range(facets):
-            a, b = c1[:, s:s + 1], s1[:, s:s + 1]
-            table[s, 0, at] = (a * c2 - b * s2).astype(BF16)
-            table[s, 1, at] = (-(b * c2 + a * s2)).astype(BF16)
-        return carry
-
-    late = []
-
-    def spread(s, p, e, d):
-        ref = full.at[s, p]
-        copy = remote(ref, ref, gc_send.at[e, d], gc_recv.at[e, d], facet=partner)
-        copy.start()
-        late.append(copy)
-
-    def across(p, e):
-        ref = full.at[q, p]
-        out = []
+        full[z, c, q] = piece.astype(BF16)
+
+    def up_copy(e):
+        ref = full.at[z, :, q]
+        return remote(ref, ref, gz_send.at[e - 1], gz_recv.at[e - 1], slab=z ^ e)
+
+    def across_copy(e, d):
+        ref = full.at[z ^ e, :, q]
+        return remote(ref, ref, gx_send.at[e, d - 1], gx_recv.at[e, d - 1], facet=at_chip(d))
+
+    def spread_copy(e, d):
+        ref = full.at[z ^ e, :, at_chip(d)]
+        return remote(ref, ref, gc_send.at[e, d], gc_recv.at[e, d], facet=partner)
+
+    def hand_on(e):
+        for d in range(chips - 1, 0, -1):
+            across_copy(e, d).start()
+        spread_copy(e, 0).start()
+
+    def relay(e):
         for d in range(1, chips):
-            copy = remote(ref, ref, gx_send.at[e, d - 1], gx_recv.at[e, d - 1], facet=at_chip(d))
-            copy.start()
-            out.append(copy)
-        return out
-
-    own = full.at[q, z]
-    g_copies = []
-    for e in range(1, slabs):
-        copy = remote(own, own, gz_send.at[e - 1], gz_recv.at[e - 1], slab=at_slab(e))
-        copy.start()
-        g_copies.append(copy)
-    a_copies = [across(z, 0)]
-    spread(q, z, 0, 0)
-    tiles = local // tile
-    done = 0
-    for e in range(1, slabs):
-        share = (e * tiles) // slabs
-        lax.fori_loop(done, share, table_step, 0)
-        done = share
-        g_copies[e - 1].wait_recv()
-        a_copies.append(across(from_slab(e), e))
-        spread(q, from_slab(e), e, 0)
-    lax.fori_loop(done, tiles, table_step, 0)
-
-    def update_pass(which, begin, end):
+            across_copy(e, d).wait_recv()
+            spread_copy(e, d).start()
+
+    tile = min(local, 256)
+
+    def update_pass(e, begin, end):
+        p = z ^ e
+        for d in range(chips):
+            spread_copy(e, d).wait_recv()
+
         def step(i, carry):
             at = pl.ds(pl.multiple_of(i * tile, tile), tile)
-            real = imag = None
-            for s in which:
-                tab_real, tab_imag = table[s, 0, at], table[s, 1, at]
-                re = jnp.concatenate([full[s, p, 0] for p in range(slabs)], axis=0)
-                im = jnp.concatenate([full[s, p, 1] for p in range(slabs)], axis=0)
-                dr = dot(tab_real, re) + dot(tab_imag, im)
-                di = dot(tab_real, im) - dot(tab_imag, re)
-                real = dr if real is None else real + dr
-                imag = di if imag is None else imag + di
+            data = full[p].reshape(2 * span, width)
+            imag = dot(table[p, at, 0:2 * span], data)
+            real = dot(table[p, at, span:3 * span], data)
             if not begin:
                 real += update_ref[0, at]
                 imag += update_ref[1, at]
@@ -382,30 +395,33 @@
             update_ref[1, at] = imag * back if end else imag
             return carry
 
-        lax.fori_loop(0, tiles, step, 0)
-
-    def relay(e):
-        for d in range(1, chips):
-            a_copies[e][d - 1].wait_recv()
-            spread(from_chip(d), from_slab(e), e, d)
-
+        lax.fori_loop(0, local // tile, step, 0)
+
+    for e in range(1, slabs):
+        up_copy(e).start()
+    hand_on(0)
+    lax.fori_loop(0, slabs, table_band, 0)
+    order = list(range(1, slabs))
+    order = order[0:1] + order[:0:-1]
+    for e in order[0:1]:
+        up_copy(e).wait_recv()
+        hand_on(e)
     relay(0)
-    update_pass([q], True, False)
-    for e in range(1, slabs - 1):
-        relay(e)
-    for copy in late[:slabs]:
-        copy.wait_recv()
-    update_pass([partner], False, False)
-    relay(slabs - 1)
-    update_pass([from_chip(d) for d in range(1, chips)], False, False)
-    for copy in late[slabs:]:
-        copy.wait_recv()
-    update_pass([from_chip(d) + 1 - 2 * core for d in range(1, chips)], False, True)
-    for copy in g_copies + late:
-        copy.wait_send()
-    for group in a_copies:
-        for copy in group:
-            copy.wait_send()
+    for e in order[1:]:
+        up_copy(e).wait_recv()
+        hand_on(e)
+    order = [0] + order
+    for k, e in enumerate(order):
+        if k + 1 < slabs:
+            relay(order[k + 1])
+        update_pass(e, k == 0, k == slabs - 1)
+    for e in range(slabs):
+        if e:
+            up_copy(e).wait_send()
+        for d in range(chips):
+            if d:
+                across_copy(e, d).wait_send()
+            spread_copy(e, d).wait_send()
 
 
 def fused(offset, subs, slab, cells, values, weights, slabs, facets):
@@ -419,7 +435,7 @@
         functools.partial(
             fused_kernel, 1.0 / math.sqrt(local * slabs * facets), 1.0 / math.sqrt(subs.shape[0] * SG)
         ),
-        in_specs=[pl.BlockSpec(memory_space=pltpu.SMEM)] * 2 + [vmem] * 6,
+        in_specs=[pl.BlockSpec(memory_space=pltpu.SMEM)] * 2 + [vmem] + [pl.BlockSpec(memory_space=pltpu.HBM)] * 4,
         out_specs=[vmem, vmem],
         out_shape=[
             jax.ShapeDtypeStruct((2, band, width), F32),
@@ -427,28 +443,34 @@
         ],
         scratch_shapes=[
             pltpu.VMEM((2, local, width), BF16),
+            pltpu.VMEM((2, local, width), BF16),
+            pltpu.VMEM(cells.shape, jnp.int32),
+            pltpu.VMEM(values.shape, F32),
+            pltpu.VMEM(weights.shape, F32),
             pltpu.VMEM((8, 128), jnp.int32),
-            pltpu.VMEM((2, SG, local), F32),
-            pltpu.VMEM((2, SG, local), F32),
-            pltpu.VMEM((chips, 2, SG, width), F32),
-            pltpu.VMEM((chips - 1, 2, SG, width), BF16),
-            pltpu.VMEM((chips - 1, 2, SG, width), BF16),
+            pltpu.VMEM((2, 2, 16, local), F32),
+            pltpu.VMEM((2, chips * (band // 16), local), F32),
+            pltpu.VMEM((slabs, 2, chips * band, width), F32),
+            pltpu.VMEM((slabs, chips - 1, 2, band, width), BF16),
+            pltpu.VMEM((slabs, chips - 1, 2, band, width), BF16),
             pltpu.VMEM((slabs, 2, band, width), F32),
-            pltpu.VMEM((slabs, 2, band, width), BF16),
+            pltpu.VMEM((slabs - 1, 2, band, width), BF16),
             pltpu.VMEM((slabs - 1, 2, band, width), BF16),
             pltpu.VMEM((3 * rows, width), F32),
-            pltpu.VMEM((facets, slabs, 2, band, width), BF16),
-            pltpu.VMEM((facets, 2, local, SG), BF16),
+            pltpu.VMEM((slabs, 2, facets, band, width), BF16),
+            pltpu.VMEM((slabs, local, 3 * facets * band), BF16),
+            pltpu.VMEM((2, local // 16, facets * band), F32),
+            dma((4,)),
             dma((2,)), dma((2,)),
-            dma((chips - 1,)), dma((chips - 1,)),
+            dma((slabs, chips - 1)), dma((slabs, chips - 1)),
             dma((slabs - 1,)), dma((slabs - 1,)),
             dma((slabs - 1,)), dma((slabs - 1,)),
             dma((slabs, chips - 1)), dma((slabs, chips - 1)),
             dma((slabs, chips)), dma((slabs, chips)),
         ],
-        compiler_params=pltpu.CompilerParams(collective_id=0, has_side_effects=True, vmem_limit_bytes=36 * 1024 * 1024),
+        compiler_params=pltpu.CompilerParams(collective_id=0, has_side_effects=True, vmem_limit_bytes=48 * 1024 * 1024),
         name="fused",
-    )(subs, offset, subs[None, :], jnp.broadcast_to(offset, (8, 128)), slab, cells, values, weights)
+    )(subs, offset, jnp.broadcast_to(offset, (8, 128)), slab, cells, values, weights)
 
 
 def body(slab, facet_offset, subgrid_offset, vis_cell, vis_value, vis_weight):
@@ -460,7 +482,9 @@
     band = SG // slabs
     owned = count_sub * band // facets
     first = (facet_offset + lax.axis_index("slab") * local_rows).astype(jnp.int32)
-    if owned == band and facets % 2 == 0 and facets > 2 and slabs > 1 and band % 16 == 0:
+    chips = facets // 2
+    paired = facets == 2 * chips and chips > 1 and chips & (chips - 1) == 0 and slabs > 1 and slabs & (slabs - 1) == 0
+    if owned == band and count_sub == facets and paired and band % 16 == 0 and local_rows % 256 == 0:
         residual, update = fused(
             facet_offset, subgrid_offset, slab[:, 0], vis_cell[0], vis_value[:, 0], vis_weight[0], slabs, facets
         )

time: 59.6 us -> 51.5 us (0.86); the launches traced: 58.6 us -> 51.3 us
  Pallas kernels: 50.6 us -> 43.4 us
    pallas_call x1, Pallas kernels: 50.6 us -> 43.4 us  [fused(): pl.pallas_call(functools.partial(fused_kernel, 1.0 / math.sqrt(local * sl...]
where the time goes in v1:
time: 51.5 us; the launch traced here: 51.3 us
  Pallas kernels  43.4 us (84%)
  local copies, waits for them, and re-layouts  6.61 us (13%)
  between operations  1.31 us (3%)
    pallas_call x1, Pallas kernels, fused(): pl.pallas_call(functools.partial(fused_kernel, 1.0 / math.sqrt(local * sl...  43.4 us
    unnamed x12, local copies, waits for them, and re-layouts  6.61 us

profile of v1, /device:TPU:0, one launch (start us, length us, event | category | flops | bytes accessed | tf_op | source)
XLA Modules:
  0.0 51.3 jit_solution(11441045407012366337)
XLA Ops:
  1.3 0.0 copy-start
  1.3 1.2 %copy-done = bf16[2,1,1024,256]{3,2,1,0:T(8,128)(2,1)S(1)} copy-done((bf16[2,1,1024,256]{3,2,1,0:T(8,128)(2,1)S(1)}, bf16[2,1,1024,256]{3,2,1,0:T(8,128)(2,1)}, u32[]{:S(2)}) %copy-start) | copy-done | bytes 1048600
  2.5 0.0 copy-start.1
  2.5 0.9 %copy-done.1 = f32[2,1,1,32768]{3,2,1,0:T(1,128)S(1)} copy-done((f32[2,1,1,32768]{3,2,1,0:T(1,128)S(1)}, f32[2,1,1,32768]{3,2,1,0:T(1,128)}, u32[]{:S(2)}) %copy-start.1) | copy-done | bytes 262168
  3.5 0.0 copy-start.2
  3.5 0.9 %copy-done.2 = s32[1,1,32768]{2,1,0:T(1,128)S(1)} copy-done((s32[1,1,32768]{2,1,0:T(1,128)S(1)}, s32[1,1,32768]{2,1,0:T(1,128)}, u32[]{:S(2)}) %copy-start.2) | copy-done | bytes 131096
  4.4 0.0 copy-start.3
  4.4 0.9 %copy-done.3 = f32[1,1,32768]{2,1,0:T(1,128)S(1)} copy-done((f32[1,1,32768]{2,1,0:T(1,128)S(1)}, f32[1,1,32768]{2,1,0:T(1,128)}, u32[]{:S(2)}) %copy-start.3) | copy-done | bytes 131096
  5.3 0.0 copy-start.4
  5.3 0.7 %copy-done.4 = s32[8]{0:T(128)S(1)} copy-done((s32[8]{0:T(128)S(1)}, s32[8]{0:T(128)}, u32[]{:S(2)}) %copy-start.4) | copy-done | bytes 56
  5.9 43.4 %fused.1 = (f32[2,64,256]{2,1,0:T(8,128)S(1)}, f32[2,1024,256]{2,1,0:T(8,128)S(1)}) custom-call(s32[8]{0:T(128)S(1)} %copy-done.4, s32[1]{0:T(128)} %copy.12.offset_ref, s32[8,128]{1,0:T(8,128)S(1)} %broadcast_in_dim.2.offv_ref, bf16[2,1024,256]{2,1,0:T(8,128)(2,1)S(1)} %bitcast.13, s32[1,32768]{1,0:T(1,128)S(1)} %bitcast.16, f32[2,1,32768]{2,1,0:T(1,128)S(1)} %bitcast.14, ...), custom_call_target="tpu_custom_call" | custom-call | tf_op jit(solution)/shard_map/fused/pallas_call | solution.py:434
  49.3 0.7 %copy.13 = f32[2,1,64,256]{3,2,1,0:T(8,128)} copy(f32[2,1,64,256]{3,2,1,0:T(8,128)S(1)} %bitcast.15) | data formatting | bytes 262144
  50.0 1.3 %copy.14 = f32[2,1,1024,256]{3,2,1,0:T(8,128)} copy(f32[2,1,1024,256]{3,2,1,0:T(8,128)S(1)} %bitcast.12) | data formatting | bytes 4194304
  (1 shorter events, 0.0 us)
Async XLA Ops:
  1.3 1.2 %copy-start = (bf16[2,1,1024,256]{3,2,1,0:T(8,128)(2,1)S(1)}, bf16[2,1,1024,256]{3,2,1,0:T(8,128)(2,1)}, u32[]{:S(2)}) copy-start(bf16[2,1,1024,256]{3,2,1,0:T(8,128)(2,1)} %param.6) | copy-start | bytes 3145732
  2.5 0.9 %copy-start.1 = (f32[2,1,1,32768]{3,2,1,0:T(1,128)S(1)}, f32[2,1,1,32768]{3,2,1,0:T(1,128)}, u32[]{:S(2)}) copy-start(f32[2,1,1,32768]{3,2,1,0:T(1,128)} %param.10) | copy-start | bytes 786436
  3.5 0.9 %copy-start.2 = (s32[1,1,32768]{2,1,0:T(1,128)S(1)}, s32[1,1,32768]{2,1,0:T(1,128)}, u32[]{:S(2)}) copy-start(s32[1,1,32768]{2,1,0:T(1,128)} %param.9) | copy-start | bytes 393220
  4.4 0.9 %copy-start.3 = (f32[1,1,32768]{2,1,0:T(1,128)S(1)}, f32[1,1,32768]{2,1,0:T(1,128)}, u32[]{:S(2)}) copy-start(f32[1,1,32768]{2,1,0:T(1,128)} %param.11) | copy-start | bytes 393220
  5.3 0.7 %copy-start.4 = (s32[8]{0:T(128)S(1)}, s32[8]{0:T(128)}, u32[]{:S(2)}) copy-start(s32[8]{0:T(128)} %subs_ref.1) | copy-start | bytes 100

commit v2 on v1

--- a/solution.py
+++ b/solution.py
@@ -13,6 +13,7 @@
 UVSTEP = 16
 F32 = jnp.float32
 BF16 = jnp.bfloat16
+EARLY = 1
 
 
 def cis(turns):
@@ -160,11 +161,11 @@
 
 
 def fused_kernel(
-    scale, back, subs_ref, offset_ref, offv_ref, slab_hbm, cell_hbm, value_hbm, weight_hbm,
-    residual_ref, update_ref,
-    slab_ref, pslab, cell_ref, value_ref, weight_ref, poff, low, high, acc, cb, rx, zf, zb, rz, sums, full,
+    scale, offset_ref, subs_hbm, slab_hbm, cell_hbm, value_hbm, weight_hbm,
+    residual_ref, update_ref, last_ref, last_table,
+    subs_ref, slab_ref, cell_ref, value_ref, weight_ref, low, high, acc, pb, rp, cb, rx, zf, zb, rz, sums, full,
     table, turn, load,
-    sw_send, sw_recv, x_send, x_recv, z_send, z_recv, gz_send, gz_recv, gx_send, gx_recv, gc_send, gc_recv,
+    p_send, p_recv, x_send, x_recv, z_send, z_recv, gz_send, gz_recv, gx_send, gx_recv, gc_send, gc_recv,
 ):
     facets, slabs = lax.axis_size("facet"), lax.axis_size("slab")
     q, z = lax.axis_index("facet"), lax.axis_index("slab")
@@ -194,29 +195,33 @@
     loads = [
         pltpu.make_async_copy(src, dst, load.at[i])
         for i, (src, dst) in enumerate(
-            [(slab_hbm, slab_ref), (cell_hbm, cell_ref), (value_hbm, value_ref), (weight_hbm, weight_ref)]
+            [
+                (subs_hbm, subs_ref), (slab_hbm, slab_ref),
+                (cell_hbm, cell_ref), (value_hbm, value_ref), (weight_hbm, weight_ref),
+            ]
         )
     ]
     for copy in loads:
         copy.start()
 
+    loads[0].wait()
     first = offset_ref[0] + z * local
     line = lax.broadcasted_iota(jnp.int32, (16, local), 1)
 
-    def build_low(places, slot):
-        c, n = cis(UVSTEP * lax.broadcasted_iota(jnp.int32, (16, local), 0) * places)
-        low[slot, 0] = c
-        low[slot, 1] = n
-
-    def partial_sum(p, places, slot, data_ref):
+    places = line + first
+    c, n = cis(UVSTEP * lax.broadcasted_iota(jnp.int32, (16, local), 0) * places)
+    low[0] = c
+    low[1] = n
+
+    def partial_sum(i, other):
         row = lax.broadcasted_iota(jnp.int32, (chips * groups, local), 0)
-        freq = UVSTEP * (band * p + 16 * (row % groups))
+        freq = UVSTEP * (band * (z ^ (slabs - 1 - i)) + 16 * (row % groups))
         for d in range(chips):
-            freq += jnp.where(row // groups == d, subs_ref[at_chip(d)], 0)
+            freq += jnp.where(row // groups == d, subs_ref[at_chip(d) ^ other], 0)
         c, n = cis(freq * places[0:1])
         high[0] = c
         high[1] = n
-        c2, s2 = low[slot, 0], low[slot, 1]
+        c2, s2 = low[0], low[1]
         cos, sin = [], []
         for g in range(chips * groups):
             c1, s1 = high[0, g:g + 1], high[1, g:g + 1]
@@ -224,54 +229,55 @@
             sin.append((s1 * c2 + c1 * s2).astype(BF16))
         cos = jnp.concatenate(cos, axis=0)
         sin = jnp.concatenate(sin, axis=0)
-        data = data_ref[...].reshape(2 * local, width)
+        data = slab_ref[...].reshape(2 * local, width)
         real = dot(jnp.concatenate([cos, sin], axis=1), data)
         imag = dot(jnp.concatenate([-sin, cos], axis=1), data)
         return real, imag
 
-    places = line + first
-    build_low(places, 0)
-    loads[0].wait()
-    pl.semaphore_wait(barrier, chips + slabs - 1)
-    swap_offset = remote(offv_ref, poff, sw_send.at[0], sw_recv.at[0], facet=partner)
-    swap_slab = remote(slab_ref, pslab, sw_send.at[1], sw_recv.at[1], facet=partner)
-    swap_offset.start()
-    swap_slab.start()
-
-    def own_part(i, carry):
-        real, imag = partial_sum(z ^ (slabs - 1 - i), places, 0, slab_ref)
+    def compute_band(i, carry):
+        real, imag = partial_sum(i, 1)
+        pb[i, 0] = real.astype(BF16)
+        pb[i, 1] = imag.astype(BF16)
+        real, imag = partial_sum(i, 0)
         acc[i, 0] = real
         acc[i, 1] = imag
         return carry
 
-    lax.fori_loop(0, slabs, own_part, 0)
-    swap_offset.wait()
-    pplaces = line + (poff[0:1, 0:1] + z * local)
-    build_low(pplaces, 1)
-    swap_slab.wait()
+    def pair_copy(i):
+        return remote(pb.at[i], rp.at[i], p_send.at[i], p_recv.at[i], facet=partner)
 
     def x_copy(i, d):
         return remote(
             cb.at[i, d - 1], rx.at[i, d - 1], x_send.at[i, d - 1], x_recv.at[i, d - 1], facet=at_chip(d)
         )
 
-    def partner_part(i, carry):
-        real, imag = partial_sum(z ^ (slabs - 1 - i), pplaces, 1, pslab)
-        for c, part in enumerate((real, imag)):
-            for d in range(1, chips):
-                at = slice(d * band, (d + 1) * band)
-                cb[i, d - 1, c] = (acc[i, c, at] + part[at]).astype(BF16)
-            zf[i, c] = acc[i, c, 0:band] + part[0:band]
+    def pair_band(i, carry):
+        pair_copy(i).wait_recv()
         for d in range(chips - 1, 0, -1):
+            at = slice(d * band, (d + 1) * band)
+            for c in range(2):
+                cb[i, d - 1, c] = (acc[i, c, at] + rp[i, c, at].astype(F32)).astype(BF16)
             x_copy(i, d).start()
+        for c in range(2):
+            zf[i, c] = acc[i, c, 0:band] + rp[i, c, 0:band].astype(F32)
         return carry
 
-    lax.fori_loop(0, slabs, partner_part, 0)
+    loads[1].wait()
+    early = min(EARLY, slabs)
+    lax.fori_loop(0, early, compute_band, 0)
+    pl.semaphore_wait(barrier, chips + slabs - 1)
+    for i in range(early):
+        pair_copy(i).start()
+    for i in range(slabs):
+        if i + early < slabs:
+            compute_band(i + early, 0)
+            pair_copy(i + early).start()
+        pair_band(i, 0)
 
     rows = sums.shape[0] // 3
     count = cell_ref.shape[1]
     chunk = min(count, 2048)
-    for copy in loads[1:]:
+    for copy in loads[2:]:
         copy.wait()
     sums[...] = jnp.zeros_like(sums)
 
@@ -299,9 +305,9 @@
 
     span = facets * band
 
-    def table_band(p, carry):
+    def table_band(e, carry):
         lane = lax.broadcasted_iota(jnp.int32, (16, span), 1)
-        freq = UVSTEP * (band * p + lane % band)
+        freq = UVSTEP * (band * (z ^ e) + lane % band)
         for s in range(facets):
             freq += jnp.where(lane // band == s, subs_ref[s], 0)
         c2, s2 = cis(freq * lax.broadcasted_iota(jnp.int32, (16, span), 0))
@@ -314,9 +320,10 @@
             c1, s1 = turn[0, pl.ds(g, 1)], turn[1, pl.ds(g, 1)]
             sin = (s1 * c2 + c1 * s2).astype(BF16)
             at = pl.ds(pl.multiple_of(g * 16, 16), 16)
-            table[p, at, 0:span] = sin
-            table[p, at, span:2 * span] = (c1 * c2 - s1 * s2).astype(BF16)
-            table[p, at, 2 * span:3 * span] = -sin
+            into = last_table if isinstance(e, int) else table.at[e]
+            into[at, 0:span] = sin
+            into[at, span:2 * span] = (c1 * c2 - s1 * s2).astype(BF16)
+            into[at, 2 * span:3 * span] = -sin
             return inner
 
         lax.fori_loop(0, local // 16, step, 0)
@@ -352,18 +359,18 @@
             model += rz[i, c].astype(F32)
         piece = sums[c * rows:c * rows + band] - sums[2 * rows:2 * rows + band] * (model * scale)
         residual_ref[c] = piece
-        full[z, c, q] = piece.astype(BF16)
+        full[0, c, q] = piece.astype(BF16)
 
     def up_copy(e):
-        ref = full.at[z, :, q]
-        return remote(ref, ref, gz_send.at[e - 1], gz_recv.at[e - 1], slab=z ^ e)
+        ref = full.at[0, :, q]
+        return remote(ref, full.at[e, :, q], gz_send.at[e - 1], gz_recv.at[e - 1], slab=z ^ e)
 
     def across_copy(e, d):
-        ref = full.at[z ^ e, :, q]
+        ref = full.at[e, :, q]
         return remote(ref, ref, gx_send.at[e, d - 1], gx_recv.at[e, d - 1], facet=at_chip(d))
 
     def spread_copy(e, d):
-        ref = full.at[z ^ e, :, at_chip(d)]
+        ref = full.at[e, :, at_chip(d)]
         return remote(ref, ref, gc_send.at[e, d], gc_recv.at[e, d], facet=partner)
 
     def hand_on(e):
@@ -378,21 +385,21 @@
 
     tile = min(local, 256)
 
-    def update_pass(e, begin, end):
-        p = z ^ e
+    def gathered(e):
         for d in range(chips):
             spread_copy(e, d).wait_recv()
 
+    def update_pass(e, begin):
         def step(i, carry):
             at = pl.ds(pl.multiple_of(i * tile, tile), tile)
-            data = full[p].reshape(2 * span, width)
-            imag = dot(table[p, at, 0:2 * span], data)
-            real = dot(table[p, at, span:3 * span], data)
+            data = full[e].reshape(2 * span, width)
+            imag = dot(table[e, at, 0:2 * span], data)
+            real = dot(table[e, at, span:3 * span], data)
             if not begin:
                 real += update_ref[0, at]
                 imag += update_ref[1, at]
-            update_ref[0, at] = real * back if end else real
-            update_ref[1, at] = imag * back if end else imag
+            update_ref[0, at] = real
+            update_ref[1, at] = imag
             return carry
 
         lax.fori_loop(0, local // tile, step, 0)
@@ -400,21 +407,26 @@
     for e in range(1, slabs):
         up_copy(e).start()
     hand_on(0)
-    lax.fori_loop(0, slabs, table_band, 0)
-    order = list(range(1, slabs))
-    order = order[0:1] + order[:0:-1]
-    for e in order[0:1]:
+    order = [0] + sorted(range(1, slabs), key=lambda e: (e != 1, -e))
+    last = order[-1]
+    lax.fori_loop(0, last, table_band, 0)
+    lax.fori_loop(last + 1, slabs, table_band, 0)
+    table_band(last, 0)
+    for k, e in enumerate(order[1:]):
         up_copy(e).wait_recv()
         hand_on(e)
-    relay(0)
-    for e in order[1:]:
-        up_copy(e).wait_recv()
-        hand_on(e)
-    order = [0] + order
+        if k == 0:
+            relay(0)
     for k, e in enumerate(order):
         if k + 1 < slabs:
             relay(order[k + 1])
-        update_pass(e, k == 0, k == slabs - 1)
+        gathered(e)
+        if e == last:
+            last_ref[...] = full[e]
+        else:
+            update_pass(e, k == 0)
+    for i in range(slabs):
+        pair_copy(i).wait_send()
     for e in range(slabs):
         if e:
             up_copy(e).wait_send()
@@ -424,6 +436,34 @@
             spread_copy(e, d).wait_send()
 
 
+def finish_kernel(back, piece_ref, part_ref, last_ref, table_ref, residual_ref, update_ref, buffer, sent):
+    dot = functools.partial(jnp.dot, preferred_element_type=F32)
+    _, local, width = part_ref.shape
+    span = table_ref.shape[1] // 3
+    tiles, _, tile, _ = buffer.shape
+    out = pltpu.make_async_copy(piece_ref, residual_ref, sent.at[tiles])
+    out.start()
+
+    def put(i):
+        at = pl.ds(pl.multiple_of(i * tile, tile), tile)
+        return pltpu.make_async_copy(buffer.at[i], update_ref.at[:, at], sent.at[i])
+
+    def step(i, carry):
+        at = pl.ds(pl.multiple_of(i * tile, tile), tile)
+        data = last_ref[...].reshape(2 * span, width)
+        imag = dot(table_ref[at, 0:2 * span], data)
+        real = dot(table_ref[at, span:3 * span], data)
+        buffer[i, 0] = (real + part_ref[0, at]) * back
+        buffer[i, 1] = (imag + part_ref[1, at]) * back
+        put(i).start()
+        return carry
+
+    lax.fori_loop(0, tiles, step, 0)
+    for i in range(tiles):
+        put(i).wait()
+    out.wait()
+
+
 def fused(offset, subs, slab, cells, values, weights, slabs, facets):
     _, local, width = slab.shape
     band = SG // slabs
@@ -431,26 +471,28 @@
     rows = -(-band // 16) * 16
     vmem = pl.BlockSpec(memory_space=pltpu.VMEM)
     dma = pltpu.SemaphoreType.DMA
-    return pl.pallas_call(
-        functools.partial(
-            fused_kernel, 1.0 / math.sqrt(local * slabs * facets), 1.0 / math.sqrt(subs.shape[0] * SG)
-        ),
-        in_specs=[pl.BlockSpec(memory_space=pltpu.SMEM)] * 2 + [vmem] + [pl.BlockSpec(memory_space=pltpu.HBM)] * 4,
-        out_specs=[vmem, vmem],
+    span = facets * band
+    piece, part, last, last_table = pl.pallas_call(
+        functools.partial(fused_kernel, 1.0 / math.sqrt(local * slabs * facets)),
+        in_specs=[pl.BlockSpec(memory_space=pltpu.SMEM)] + [pl.BlockSpec(memory_space=pltpu.HBM)] * 5,
+        out_specs=[vmem] * 4,
         out_shape=[
             jax.ShapeDtypeStruct((2, band, width), F32),
             jax.ShapeDtypeStruct((2, local, width), F32),
+            jax.ShapeDtypeStruct((2, facets, band, width), BF16),
+            jax.ShapeDtypeStruct((local, 3 * span), BF16),
         ],
         scratch_shapes=[
-            pltpu.VMEM((2, local, width), BF16),
+            pltpu.SMEM(subs.shape, jnp.int32),
             pltpu.VMEM((2, local, width), BF16),
             pltpu.VMEM(cells.shape, jnp.int32),
             pltpu.VMEM(values.shape, F32),
             pltpu.VMEM(weights.shape, F32),
-            pltpu.VMEM((8, 128), jnp.int32),
-            pltpu.VMEM((2, 2, 16, local), F32),
+            pltpu.VMEM((2, 16, local), F32),
             pltpu.VMEM((2, chips * (band // 16), local), F32),
             pltpu.VMEM((slabs, 2, chips * band, width), F32),
+            pltpu.VMEM((slabs, 2, chips * band, width), BF16),
+            pltpu.VMEM((slabs, 2, chips * band, width), BF16),
             pltpu.VMEM((slabs, chips - 1, 2, band, width), BF16),
             pltpu.VMEM((slabs, chips - 1, 2, band, width), BF16),
             pltpu.VMEM((slabs, 2, band, width), F32),
@@ -458,19 +500,32 @@
             pltpu.VMEM((slabs - 1, 2, band, width), BF16),
             pltpu.VMEM((3 * rows, width), F32),
             pltpu.VMEM((slabs, 2, facets, band, width), BF16),
-            pltpu.VMEM((slabs, local, 3 * facets * band), BF16),
-            pltpu.VMEM((2, local // 16, facets * band), F32),
-            dma((4,)),
-            dma((2,)), dma((2,)),
+            pltpu.VMEM((slabs, local, 3 * span), BF16),
+            pltpu.VMEM((2, local // 16, span), F32),
+            dma((5,)),
+            dma((slabs,)), dma((slabs,)),
             dma((slabs, chips - 1)), dma((slabs, chips - 1)),
             dma((slabs - 1,)), dma((slabs - 1,)),
             dma((slabs - 1,)), dma((slabs - 1,)),
             dma((slabs, chips - 1)), dma((slabs, chips - 1)),
             dma((slabs, chips)), dma((slabs, chips)),
         ],
-        compiler_params=pltpu.CompilerParams(collective_id=0, has_side_effects=True, vmem_limit_bytes=48 * 1024 * 1024),
+        compiler_params=pltpu.CompilerParams(collective_id=0, has_side_effects=True, vmem_limit_bytes=40 * 1024 * 1024),
         name="fused",
-    )(subs, offset, jnp.broadcast_to(offset, (8, 128)), slab, cells, values, weights)
+    )(offset, *[pltpu.with_memory_space_constraint(x, pltpu.HBM) for x in (subs, slab, cells, values, weights)])
+    tiles = local // min(local, 256)
+    return pl.pallas_call(
+        functools.partial(finish_kernel, 1.0 / math.sqrt(subs.shape[0] * SG)),
+        in_specs=[vmem] * 4,
+        out_specs=[pl.BlockSpec(memory_space=pltpu.HBM)] * 2,
+        out_shape=[
+            jax.ShapeDtypeStruct((2, band, width), F32),
+            jax.ShapeDtypeStruct((2, local, width), F32),
+        ],
+        scratch_shapes=[pltpu.VMEM((tiles, 2, local // tiles, width), F32), dma((tiles + 1,))],
+        compiler_params=pltpu.CompilerParams(vmem_limit_bytes=8 * 1024 * 1024),
+        name="finish",
+    )(piece, part, last, last_table)
 
 
 def body(slab, facet_offset, subgrid_offset, vis_cell, vis_value, vis_weight):

time: 51.5 us -> 45 us (0.87)
  local copies, waits for them, and re-layouts: 6.61 us -> 0 us
    unnamed x12 -> x0, local copies, waits for them, and re-layouts: 6.61 us -> none
    pallas_call x0 -> x1, Pallas kernels: none -> 2.6 us  [fused(): pl.pallas_call(functools.partial(finish_kernel, 1.0 / math.sqrt(subs.shap...]
    pallas_call x1, Pallas kernels: 43.4 us -> 41 us  [fused(): pl.pallas_call(functools.partial(fused_kernel, 1.0 / math.sqrt(local * sl...]
where the time goes in v2:
time: 45 us; the launch traced here: 44.9 us
  Pallas kernels  43.6 us (97%)
  between operations  1.28 us (3%)
    pallas_call x1, Pallas kernels, fused(): pl.pallas_call(functools.partial(fused_kernel, 1.0 / math.sqrt(local * sl...  41 us
    pallas_call x1, Pallas kernels, fused(): pl.pallas_call(functools.partial(finish_kernel, 1.0 / math.sqrt(subs.shap...  2.6 us

profile of v2, /device:TPU:0, one launch (start us, length us, event | category | flops | bytes accessed | tf_op | source)
XLA Modules:
  0.0 44.9 jit_solution(12564755064461633457)
XLA Ops:
  1.3 41.0 %fused.1 = (f32[2,64,256]{2,1,0:T(8,128)S(1)}, f32[2,1024,256]{2,1,0:T(8,128)S(1)}, bf16[2,8,64,256]{3,2,1,0:T(8,128)(2,1)S(1)}, bf16[1024,1536]{1,0:T(8,128)(2,1)S(1)}) custom-call(s32[1]{0:T(128)S(6)} %copy.10.offset_ref, s32[8]{0:T(128)} %subs_hbm.1, bf16[2,1024,256]{2,1,0:T(8,128)(2,1)} %bitcast.10, s32[1,32768]{1,0:T(1,128)} %bitcast.12, ...), custom_call_target="tpu_custom_call" | custom-call | tf_op jit(solution)/shard_map/fused/pallas_call | solution.py:475
  42.3 2.6 %finish.1 = (f32[2,64,256]{2,1,0:T(8,128)}, f32[2,1024,256]{2,1,0:T(8,128)}) custom-call(f32[2,64,256]{2,1,0:T(8,128)S(1)} %get-tuple-element.8.piece_ref, f32[2,1024,256]{2,1,0:T(8,128)S(1)} %get-tuple-element.9.part_ref, bf16[2,8,64,256]{3,2,1,0:T(8,128)(2,1)S(1)} %get-tuple-element.10.last_ref, bf16[1024,1536]{1,0:T(8,128)(2,1)S(1)} %get-tuple-element.11.table_ref), custom_call_target="tpu_custom_call" | custom-call | tf_op jit(solution)/shard_map/finish/pallas_call | solution.py:517

commit v3 on v2

--- a/solution.py
+++ b/solution.py
@@ -13,7 +13,6 @@
 UVSTEP = 16
 F32 = jnp.float32
 BF16 = jnp.bfloat16
-EARLY = 1
 
 
 def cis(turns):
@@ -163,9 +162,9 @@
 def fused_kernel(
     scale, offset_ref, subs_hbm, slab_hbm, cell_hbm, value_hbm, weight_hbm,
     residual_ref, update_ref, last_ref, last_table,
-    subs_ref, slab_ref, cell_ref, value_ref, weight_ref, low, high, acc, pb, rp, cb, rx, zf, zb, rz, sums, full,
+    subs_ref, slab_ref, cell_ref, value_ref, weight_ref, low, high, acc, pb, rp, cb, rx, dg, zd, zf, zb, rz, sums, flat, full,
     table, turn, load,
-    p_send, p_recv, x_send, x_recv, z_send, z_recv, gz_send, gz_recv, gx_send, gx_recv, gc_send, gc_recv,
+    p_send, p_recv, x_send, x_recv, d_send, d_recv, z_send, z_recv, gz_send, gz_recv, gx_send, gx_recv, gc_send, gc_recv,
 ):
     facets, slabs = lax.axis_size("facet"), lax.axis_size("slab")
     q, z = lax.axis_index("facet"), lax.axis_index("slab")
@@ -175,6 +174,8 @@
     _, local, width = slab_ref.shape
     band = SG // slabs
     groups = band // 16
+    parts = x_send.shape[1]
+    share = band // parts
     dot = functools.partial(jnp.dot, preferred_element_type=F32)
 
     def at_chip(d):
@@ -230,53 +231,92 @@
         cos = jnp.concatenate(cos, axis=0)
         sin = jnp.concatenate(sin, axis=0)
         data = slab_ref[...].reshape(2 * local, width)
-        real = dot(jnp.concatenate([cos, sin], axis=1), data)
-        imag = dot(jnp.concatenate([-sin, cos], axis=1), data)
-        return real, imag
-
-    def compute_band(i, carry):
-        real, imag = partial_sum(i, 1)
-        pb[i, 0] = real.astype(BF16)
-        pb[i, 1] = imag.astype(BF16)
-        real, imag = partial_sum(i, 0)
-        acc[i, 0] = real
-        acc[i, 1] = imag
-        return carry
+        both = jnp.concatenate(
+            [jnp.concatenate([cos, sin], axis=1), jnp.concatenate([-sin, cos], axis=1)], axis=0
+        )
+        return dot(both, data).reshape(2, chips * band, width)
+
+    def compute_other(i):
+        pb[i] = partial_sum(i, 1).astype(BF16)
+
+    def compute_own(i):
+        acc[i] = partial_sum(i, 0)
 
     def pair_copy(i):
         return remote(pb.at[i], rp.at[i], p_send.at[i], p_recv.at[i], facet=partner)
 
-    def x_copy(i, d):
+    def part(h):
+        return slice(h * share, (h + 1) * share)
+
+    def x_copy(i, h, d):
         return remote(
-            cb.at[i, d - 1], rx.at[i, d - 1], x_send.at[i, d - 1], x_recv.at[i, d - 1], facet=at_chip(d)
-        )
-
-    def pair_band(i, carry):
+            cb.at[i, d - 1, :, part(h)], rx.at[i, d - 1, :, part(h)],
+            x_send.at[i, h, d - 1], x_recv.at[i, h, d - 1], facet=at_chip(d),
+        )
+
+    own, far = slabs - 1, chips - 1
+    routed = [i for i in range(own) if (own - i) % 2 == 1]
+
+    def d_copy(i, h):
+        k = routed.index(i)
+        return remote(
+            cb.at[i, far - 1, :, part(h)], zd.at[k, :, part(h)], d_send.at[k, h], d_recv.at[k, h], slab=z ^ (own - i)
+        )
+
+    def ways(i):
+        return [d for d in range(far, 0, -1) if d != far or i not in routed]
+
+    def x_send_part(i, h):
+        for d in ways(i):
+            if i != own or d != far:
+                x_copy(i, h, d).start()
+
+    def pair_band(i):
         pair_copy(i).wait_recv()
-        for d in range(chips - 1, 0, -1):
+        for d in range(far, 0, -1):
             at = slice(d * band, (d + 1) * band)
             for c in range(2):
-                cb[i, d - 1, c] = (acc[i, c, at] + rp[i, c, at].astype(F32)).astype(BF16)
-            x_copy(i, d).start()
+                total = acc[i, c, at] + rp[i, c, at].astype(F32)
+                if i == own and d == far:
+                    dg[c] = total
+                else:
+                    cb[i, d - 1, c] = total.astype(BF16)
+        x_send_part(i, 0)
+        if i in routed:
+            for h in range(parts):
+                d_copy(i, h).start()
         for c in range(2):
             zf[i, c] = acc[i, c, 0:band] + rp[i, c, 0:band].astype(F32)
-        return carry
+
+    def send_far(h):
+        for i in routed:
+            d_copy(i, h).wait()
+        for c in range(2):
+            total = dg[c, part(h)]
+            for k in range(len(routed)):
+                total += zd[k, c, part(h)].astype(F32)
+            cb[own, far - 1, c, part(h)] = total.astype(BF16)
+        x_copy(own, h, far).start()
 
     loads[1].wait()
-    early = min(EARLY, slabs)
-    lax.fori_loop(0, early, compute_band, 0)
+    compute_other(0)
     pl.semaphore_wait(barrier, chips + slabs - 1)
-    for i in range(early):
-        pair_copy(i).start()
+    pair_copy(0).start()
+    compute_own(0)
     for i in range(slabs):
-        if i + early < slabs:
-            compute_band(i + early, 0)
-            pair_copy(i + early).start()
-        pair_band(i, 0)
-
-    rows = sums.shape[0] // 3
+        if i + 1 < slabs:
+            compute_other(i + 1)
+            pair_copy(i + 1).start()
+        pair_band(i)
+        if i + 1 < slabs:
+            compute_own(i + 1)
+    if parts == 2:
+        for i in range(own - 1):
+            x_send_part(i, 1)
+
+    rows = sums.shape[1] // 3
     count = cell_ref.shape[1]
-    chunk = min(count, 2048)
+    chunk = min(count, 8192)
     for copy in loads[2:]:
         copy.wait()
     sums[...] = jnp.zeros_like(sums)
@@ -300,16 +340,17 @@
             [jnp.where(row == lines + jnp.asarray(g, BF16), t, zero) for t in terms for g in range(0, rows, 16)],
             axis=0,
         )
-        sums[...] += lax.dot_general(left, hot, (((1,), (1,)), ((), ())), preferred_element_type=F32)
+        sums[...] += lax.dot_general(hot, left, (((1,), (1,)), ((), ())), preferred_element_type=F32)
         return carry
 
-    span = facets * band
-
-    def table_band(e, carry):
+    span = facets * share
+
+    def table_band(t, carry):
+        e, h = t // parts, t % parts
         lane = lax.broadcasted_iota(jnp.int32, (16, span), 1)
-        freq = UVSTEP * (band * (z ^ e) + lane % band)
+        freq = UVSTEP * (band * (z ^ e) + share * h + lane % share)
         for s in range(facets):
-            freq += jnp.where(lane // band == s, subs_ref[s], 0)
+            freq += jnp.where(lane // share == s, subs_ref[s], 0)
         c2, s2 = cis(freq * lax.broadcasted_iota(jnp.int32, (16, span), 0))
         far = first + 16 * lax.broadcasted_iota(jnp.int32, (local // 16, span), 0)
         c, n = cis(freq[0:1] * far)
@@ -320,7 +361,7 @@
             c1, s1 = turn[0, pl.ds(g, 1)], turn[1, pl.ds(g, 1)]
             sin = (s1 * c2 + c1 * s2).astype(BF16)
             at = pl.ds(pl.multiple_of(g * 16, 16), 16)
-            into = last_table if isinstance(e, int) else table.at[e]
+            into = last_table if isinstance(t, int) else table.at[e, h]
             into[at, 0:span] = sin
             into[at, span:2 * span] = (c1 * c2 - s1 * s2).astype(BF16)
             into[at, 2 * span:3 * span] = -sin
@@ -330,71 +371,85 @@
         return carry
 
     chunks = count // chunk
-    cuts = [0, (6 * chunks) // 16, (9 * chunks) // 16, (13 * chunks) // 16, chunks]
-    cuts = [cuts[min(i, 4)] for i in range(slabs)] + [chunks]
-
-    def z_copy(i):
-        return remote(zb.at[i], rz.at[i], z_send.at[i], z_recv.at[i], slab=z ^ (slabs - 1 - i))
-
-    model = []
-    for i in range(slabs):
-        lax.fori_loop(cuts[i], cuts[i + 1], grid_step, 0)
+
+    def grid(i):
+        lax.fori_loop((i * chunks) // slabs, ((i + 1) * chunks) // slabs, grid_step, 0)
+
+    def z_copy(i, h):
+        return remote(
+            zb.at[i, :, part(h)], rz.at[i, :, part(h)], z_send.at[i, h], z_recv.at[i, h], slab=z ^ (slabs - 1 - i)
+        )
+
+    def reduce_part(i, h):
+        for d in ways(i):
+            x_copy(i, h, d).wait()
+        for c in range(2):
+            total = zf[i, c, part(h)]
+            for d in ways(i):
+                total += rx[i, d - 1, c, part(h)].astype(F32)
+            if i < slabs - 1:
+                zb[i, c, part(h)] = total.astype(BF16)
+            else:
+                zf[i, c, part(h)] = total
+        if i < slabs - 1:
+            z_copy(i, h).start()
+
+    def residual_part(h):
+        for i in range(slabs - 1):
+            z_copy(i, h).wait()
+        for c in range(2):
+            model = zf[slabs - 1, c, part(h)]
+            for i in range(slabs - 1):
+                model += rz[i, c, part(h)].astype(F32)
+            at = h * share
+            piece = flat[c * rows + at:c * rows + at + share]
+            piece -= flat[2 * rows + at:2 * rows + at + share] * (model * scale)
+            residual_ref[c, part(h)] = piece
+            full[0, h, c, q] = piece.astype(BF16)
+
+    def up_copy(e, h):
+        return remote(
+            full.at[0, h, :, q], full.at[e, h, :, q], gz_send.at[e - 1, h], gz_recv.at[e - 1, h],
+            slab=z ^ e,
+        )
+
+    def across_copy(e, h, d):
+        ref = full.at[e, h, :, q]
+        return remote(ref, ref, gx_send.at[e, h, d - 1], gx_recv.at[e, h, d - 1], facet=at_chip(d))
+
+    def spread_copy(e, h, d):
+        ref = full.at[e, h, :, at_chip(d)]
+        return remote(ref, ref, gc_send.at[e, h, d], gc_recv.at[e, h, d], facet=partner)
+
+    def hand_on(e, h):
+        if e:
+            up_copy(e, h).wait_recv()
+        else:
+            for away in order[1:]:
+                up_copy(away, h).start()
         for d in range(chips - 1, 0, -1):
-            x_copy(i, d).wait()
-        for c in range(2):
-            total = zf[i, c]
-            for d in range(1, chips):
-                total += rx[i, d - 1, c].astype(F32)
-            if i < slabs - 1:
-                zb[i, c] = total.astype(BF16)
-            else:
-                zf[i, c] = total
-        if i < slabs - 1:
-            z_copy(i).start()
-    for i in range(slabs - 1):
-        z_copy(i).wait()
-    for c in range(2):
-        model = zf[slabs - 1, c]
-        for i in range(slabs - 1):
-            model += rz[i, c].astype(F32)
-        piece = sums[c * rows:c * rows + band] - sums[2 * rows:2 * rows + band] * (model * scale)
-        residual_ref[c] = piece
-        full[0, c, q] = piece.astype(BF16)
-
-    def up_copy(e):
-        ref = full.at[0, :, q]
-        return remote(ref, full.at[e, :, q], gz_send.at[e - 1], gz_recv.at[e - 1], slab=z ^ e)
-
-    def across_copy(e, d):
-        ref = full.at[e, :, q]
-        return remote(ref, ref, gx_send.at[e, d - 1], gx_recv.at[e, d - 1], facet=at_chip(d))
-
-    def spread_copy(e, d):
-        ref = full.at[e, :, at_chip(d)]
-        return remote(ref, ref, gc_send.at[e, d], gc_recv.at[e, d], facet=partner)
-
-    def hand_on(e):
-        for d in range(chips - 1, 0, -1):
-            across_copy(e, d).start()
-        spread_copy(e, 0).start()
-
-    def relay(e):
+            across_copy(e, h, d).start()
+        spread_copy(e, h, 0).start()
+
+    def relay(e, h):
         for d in range(1, chips):
-            across_copy(e, d).wait_recv()
-            spread_copy(e, d).start()
-
-    tile = min(local, 256)
-
-    def gathered(e):
+            across_copy(e, h, d).wait_recv()
+            spread_copy(e, h, d).start()
+
+    tile = min(local, 1024)
+
+    def gathered(e, h):
         for d in range(chips):
-            spread_copy(e, d).wait_recv()
-
-    def update_pass(e, begin):
+            spread_copy(e, h, d).wait_recv()
+
+    def update_pass(e, h, begin=False):
+        gathered(e, h)
+
         def step(i, carry):
             at = pl.ds(pl.multiple_of(i * tile, tile), tile)
-            data = full[e].reshape(2 * span, width)
-            imag = dot(table[e, at, 0:2 * span], data)
-            real = dot(table[e, at, span:3 * span], data)
+            data = full[e, h].reshape(2 * span, width)
+            imag = dot(table[e, h, at, 0:2 * span], data)
+            real = dot(table[e, h, at, span:3 * span], data)
             if not begin:
                 real += update_ref[0, at]
                 imag += update_ref[1, at]
@@ -404,36 +459,87 @@
 
         lax.fori_loop(0, local // tile, step, 0)
 
-    for e in range(1, slabs):
-        up_copy(e).start()
-    hand_on(0)
+    def tables(begin, end):
+        final = last * parts + parts - 1
+        if begin <= final < end:
+            lax.fori_loop(begin, final, table_band, 0)
+            table_band(final, 0)
+            begin = final + 1
+        if begin < end:
+            lax.fori_loop(begin, end, table_band, 0)
+
     order = [0] + sorted(range(1, slabs), key=lambda e: (e != 1, -e))
     last = order[-1]
-    lax.fori_loop(0, last, table_band, 0)
-    lax.fori_loop(last + 1, slabs, table_band, 0)
-    table_band(last, 0)
+    units = slabs * parts
+    final = parts - 1
+
+    reduce_part(0, 0)
+    grid(0)
+    for i in range(1, own):
+        reduce_part(i, 0)
+        if i == 1:
+            send_far(0)
+            if parts == 2:
+                x_send_part(own - 1, 1)
+                x_send_part(own, 1)
+        grid(i)
+    if parts == 2:
+        send_far(1)
+        reduce_part(0, 1)
+    grid(own)
+    flat[...] = sums[...].T
+    if parts == 2:
+        for i in range(1, own - 1):
+            reduce_part(i, 1)
+    reduce_part(own, 0)
+    residual_part(0)
+    hand_on(0, 0)
+    if parts == 2:
+        reduce_part(own - 1, 1)
+        tables(0, 2)
+        reduce_part(own, 1)
+        tables(2, 3)
+        hand_on(1, 0)
+        residual_part(1)
+        hand_on(0, 1)
+        for e in order[2:-1]:
+            hand_on(e, 0)
+        relay(0, 0)
+        tables(3, 5)
+        hand_on(last, 0)
+        tables(5, units)
+        hand_on(1, 1)
+        relay(1, 0)
+        update_pass(0, 0, True)
+        for k, e in enumerate(order[2:]):
+            hand_on(e, 1)
+            if e != last:
+                relay(e, 0)
+                update_pass(order[k + 1], 0)
+        relay(last, 0)
+        relay(0, 1)
+        for e in order[2:]:
+            update_pass(e, 0)
+    else:
+        tables(0, units)
+        for e in order[1:]:
+            hand_on(e, 0)
+        relay(0, 0)
     for k, e in enumerate(order[1:]):
-        up_copy(e).wait_recv()
-        hand_on(e)
-        if k == 0:
-            relay(0)
-    for k, e in enumerate(order):
-        if k + 1 < slabs:
-            relay(order[k + 1])
-        gathered(e)
-        if e == last:
-            last_ref[...] = full[e]
-        else:
-            update_pass(e, k == 0)
+        relay(e, final)
+        update_pass(order[k], final, parts == 1 and k == 0)
+    gathered(last, final)
+    last_ref[...] = full[last, final]
     for i in range(slabs):
         pair_copy(i).wait_send()
     for e in range(slabs):
-        if e:
-            up_copy(e).wait_send()
-        for d in range(chips):
-            if d:
-                across_copy(e, d).wait_send()
-            spread_copy(e, d).wait_send()
+        for h in range(parts):
+            if e:
+                up_copy(e, h).wait_send()
+            for d in range(chips):
+                if d:
+                    across_copy(e, h, d).wait_send()
+                spread_copy(e, h, d).wait_send()
 
 
 def finish_kernel(back, piece_ref, part_ref, last_ref, table_ref, residual_ref, update_ref, buffer, sent):
@@ -471,7 +577,9 @@
     rows = -(-band // 16) * 16
     vmem = pl.BlockSpec(memory_space=pltpu.VMEM)
     dma = pltpu.SemaphoreType.DMA
-    span = facets * band
+    parts = 2 if band % 32 == 0 else 1
+    share = band // parts
+    span = facets * share
     piece, part, last, last_table = pl.pallas_call(
         functools.partial(fused_kernel, 1.0 / math.sqrt(local * slabs * facets)),
         in_specs=[pl.BlockSpec(memory_space=pltpu.SMEM)] + [pl.BlockSpec(memory_space=pltpu.HBM)] * 5,
@@ -479,7 +587,7 @@
         out_shape=[
             jax.ShapeDtypeStruct((2, band, width), F32),
             jax.ShapeDtypeStruct((2, local, width), F32),
-            jax.ShapeDtypeStruct((2, facets, band, width), BF16),
+            jax.ShapeDtypeStruct((2, facets, share, width), BF16),
             jax.ShapeDtypeStruct((local, 3 * span), BF16),
         ],
         scratch_shapes=[
@@ -495,20 +603,24 @@
             pltpu.VMEM((slabs, 2, chips * band, width), BF16),
             pltpu.VMEM((slabs, chips - 1, 2, band, width), BF16),
             pltpu.VMEM((slabs, chips - 1, 2, band, width), BF16),
+            pltpu.VMEM((2, band, width), F32),
+            pltpu.VMEM((slabs // 2, 2, band, width), BF16),
             pltpu.VMEM((slabs, 2, band, width), F32),
             pltpu.VMEM((slabs - 1, 2, band, width), BF16),
             pltpu.VMEM((slabs - 1, 2, band, width), BF16),
+            pltpu.VMEM((width, 3 * rows), F32),
             pltpu.VMEM((3 * rows, width), F32),
-            pltpu.VMEM((slabs, 2, facets, band, width), BF16),
-            pltpu.VMEM((slabs, local, 3 * span), BF16),
+            pltpu.VMEM((slabs, parts, 2, facets, share, width), BF16),
+            pltpu.VMEM((slabs, parts, local, 3 * span), BF16),
             pltpu.VMEM((2, local // 16, span), F32),
             dma((5,)),
             dma((slabs,)), dma((slabs,)),
-            dma((slabs, chips - 1)), dma((slabs, chips - 1)),
-            dma((slabs - 1,)), dma((slabs - 1,)),
-            dma((slabs - 1,)), dma((slabs - 1,)),
-            dma((slabs, chips - 1)), dma((slabs, chips - 1)),
-            dma((slabs, chips)), dma((slabs, chips)),
+            dma((slabs, parts, chips - 1)), dma((slabs, parts, chips - 1)),
+            dma((slabs // 2, parts)), dma((slabs // 2, parts)),
+            dma((slabs - 1, parts)), dma((slabs - 1, parts)),
+            dma((slabs - 1, parts)), dma((slabs - 1, parts)),
+            dma((slabs, parts, chips - 1)), dma((slabs, parts, chips - 1)),
+            dma((slabs, parts, chips)), dma((slabs, parts, chips)),
         ],
         compiler_params=pltpu.CompilerParams(collective_id=0, has_side_effects=True, vmem_limit_bytes=40 * 1024 * 1024),
         name="fused",
@@ -538,7 +650,7 @@
     owned = count_sub * band // facets
     first = (facet_offset + lax.axis_index("slab") * local_rows).astype(jnp.int32)
     chips = facets // 2
-    paired = facets == 2 * chips and chips > 1 and chips & (chips - 1) == 0 and slabs > 1 and slabs & (slabs - 1) == 0
+    paired = facets == 2 * chips and chips == 4 and slabs > 2 and slabs & (slabs - 1) == 0
     if owned == band and count_sub == facets and paired and band % 16 == 0 and local_rows % 256 == 0:
         residual, update = fused(
             facet_offset, subgrid_offset, slab[:, 0], vis_cell[0], vis_value[:, 0], vis_weight[0], slabs, facets

time: 45 us -> 43.8 us (0.973)
  Pallas kernels: 43.6 us -> 42.2 us
    pallas_call x1, Pallas kernels: 41 us -> 40.1 us  [fused(): pl.pallas_call(functools.partial(fused_kernel, 1.0 / math.sqrt(local * sl...]
    pallas_call x1, Pallas kernels: 2.6 us -> 2.05 us  [fused(): pl.pallas_call(functools.partial(finish_kernel, 1.0 / math.sqrt(subs.shap...]
where the time goes in v3:
time: 43.8 us; the launch traced here: 43.6 us
  Pallas kernels  42.2 us (96%)
  between operations  1.44 us (3%)
    pallas_call x1, Pallas kernels, fused(): pl.pallas_call(functools.partial(fused_kernel, 1.0 / math.sqrt(local * sl...  40.1 us
    pallas_call x1, Pallas kernels, fused(): pl.pallas_call(functools.partial(finish_kernel, 1.0 / math.sqrt(subs.shap...  2.05 us

profile of v3, /device:TPU:0, one launch (start us, length us, event | category | flops | bytes accessed | tf_op | source)
XLA Modules:
  0.0 43.6 jit_solution(3596102327261180926)
XLA Ops:
  1.3 40.1 %fused.1 = (f32[2,64,256]{2,1,0:T(8,128)S(1)}, f32[2,1024,256]{2,1,0:T(8,128)S(1)}, bf16[2,8,32,256]{3,2,1,0:T(8,128)(2,1)S(1)}, bf16[1024,768]{1,0:T(8,128)(2,1)S(1)}) custom-call(s32[1]{0:T(128)S(6)} %copy.10.offset_ref, s32[8]{0:T(128)} %subs_hbm.1, bf16[2,1024,256]{2,1,0:T(8,128)(2,1)} %bitcast.10, s32[1,32768]{1,0:T(1,128)} %bitcast.12, ...), custom_call_target="tpu_custom_call" | custom-call | tf_op jit(solution)/shard_map/fused/pallas_call | solution.py:583
  41.4 2.1 %finish.1 = (f32[2,64,256]{2,1,0:T(8,128)}, f32[2,1024,256]{2,1,0:T(8,128)}) custom-call(f32[2,64,256]{2,1,0:T(8,128)S(1)} %get-tuple-element.8.piece_ref, f32[2,1024,256]{2,1,0:T(8,128)S(1)} %get-tuple-element.9.part_ref, bf16[2,8,32,256]{3,2,1,0:T(8,128)(2,1)S(1)} %get-tuple-element.10.last_ref, bf16[1024,768]{1,0:T(8,128)(2,1)S(1)} %get-tuple-element.11.table_ref), custom_call_target="tpu_custom_call" | custom-call | tf_op jit(solution)/shard_map/finish/pallas_call | solution.py:629

commit v4 on v3

--- a/solution.py
+++ b/solution.py
@@ -316,7 +316,7 @@
 
     rows = sums.shape[1] // 3
     count = cell_ref.shape[1]
-    chunk = min(count, 8192)
+    chunk = min(count, 4096)
     for copy in loads[2:]:
         copy.wait()
     sums[...] = jnp.zeros_like(sums)

time: 43.8 us -> 40.4 us (0.922)
  Pallas kernels: 42.2 us -> 38.9 us
    pallas_call x1, Pallas kernels: 40.1 us -> 36.9 us  [fused(): pl.pallas_call(functools.partial(fused_kernel, 1.0 / math.sqrt(local * sl...]
where the time goes in v4:
time: 40.4 us; the launch traced here: 40.2 us
  Pallas kernels  38.9 us (96%)
  between operations  1.28 us (3%)
    pallas_call x1, Pallas kernels, fused(): pl.pallas_call(functools.partial(fused_kernel, 1.0 / math.sqrt(local * sl...  36.9 us
    pallas_call x1, Pallas kernels, fused(): pl.pallas_call(functools.partial(finish_kernel, 1.0 / math.sqrt(subs.shap...  2.06 us

profile of v4, /device:TPU:0, one launch (start us, length us, event | category | flops | bytes accessed | tf_op | source)
XLA Modules:
  0.0 40.2 jit_solution(6580394071533831351)
XLA Ops:
  1.3 36.9 %fused.1 = (f32[2,64,256]{2,1,0:T(8,128)S(1)}, f32[2,1024,256]{2,1,0:T(8,128)S(1)}, bf16[2,8,32,256]{3,2,1,0:T(8,128)(2,1)S(1)}, bf16[1024,768]{1,0:T(8,128)(2,1)S(1)}) custom-call(s32[1]{0:T(128)S(6)} %copy.10.offset_ref, s32[8]{0:T(128)} %subs_hbm.1, bf16[2,1024,256]{2,1,0:T(8,128)(2,1)} %bitcast.10, s32[1,32768]{1,0:T(1,128)} %bitcast.12, ...), custom_call_target="tpu_custom_call" | custom-call | tf_op jit(solution)/shard_map/fused/pallas_call | solution.py:583
  38.1 2.1 %finish.1 = (f32[2,64,256]{2,1,0:T(8,128)}, f32[2,1024,256]{2,1,0:T(8,128)}) custom-call(f32[2,64,256]{2,1,0:T(8,128)S(1)} %get-tuple-element.8.piece_ref, f32[2,1024,256]{2,1,0:T(8,128)S(1)} %get-tuple-element.9.part_ref, bf16[2,8,32,256]{3,2,1,0:T(8,128)(2,1)S(1)} %get-tuple-element.10.last_ref, bf16[1024,768]{1,0:T(8,128)(2,1)S(1)} %get-tuple-element.11.table_ref), custom_call_target="tpu_custom_call" | custom-call | tf_op jit(solution)/shard_map/finish/pallas_call | solution.py:629

commit v5 on v4

--- a/solution.py
+++ b/solution.py
@@ -13,6 +13,9 @@
 UVSTEP = 16
 F32 = jnp.float32
 BF16 = jnp.bfloat16
+GRID = 8192
+GRID_LATE = 0
+TILE = 1024
 
 
 def cis(turns):
@@ -161,9 +164,9 @@
 
 def fused_kernel(
     scale, offset_ref, subs_hbm, slab_hbm, cell_hbm, value_hbm, weight_hbm,
-    residual_ref, update_ref, last_ref, last_table,
+    residual_ref, update_ref, last_ref, table,
     subs_ref, slab_ref, cell_ref, value_ref, weight_ref, low, high, acc, pb, rp, cb, rx, dg, zd, zf, zb, rz, sums, flat, full,
-    table, turn, load,
+    turn, load,
     p_send, p_recv, x_send, x_recv, d_send, d_recv, z_send, z_recv, gz_send, gz_recv, gx_send, gx_recv, gc_send, gc_recv,
 ):
     facets, slabs = lax.axis_size("facet"), lax.axis_size("slab")
@@ -236,12 +239,6 @@
         )
         return dot(both, data).reshape(2, chips * band, width)
 
-    def compute_other(i):
-        pb[i] = partial_sum(i, 1).astype(BF16)
-
-    def compute_own(i):
-        acc[i] = partial_sum(i, 0)
-
     def pair_copy(i):
         return remote(pb.at[i], rp.at[i], p_send.at[i], p_recv.at[i], facet=partner)
 
@@ -255,68 +252,70 @@
         )
 
     own, far = slabs - 1, chips - 1
-    routed = [i for i in range(own) if (own - i) % 2 == 1]
+
+    def routed(i):
+        return i % 2 == 0
 
     def d_copy(i, h):
-        k = routed.index(i)
         return remote(
-            cb.at[i, far - 1, :, part(h)], zd.at[k, :, part(h)], d_send.at[k, h], d_recv.at[k, h], slab=z ^ (own - i)
+            cb.at[i, far - 1, :, part(h)], zd.at[i // 2, :, part(h)], d_send.at[i // 2, h], d_recv.at[i // 2, h],
+            slab=z ^ (own - i),
         )
 
     def ways(i):
-        return [d for d in range(far, 0, -1) if d != far or i not in routed]
+        return [d for d in range(far, 0, -1) if d != far or not routed(i)]
 
     def x_send_part(i, h):
         for d in ways(i):
             if i != own or d != far:
                 x_copy(i, h, d).start()
 
-    def pair_band(i):
+    def pair_band(i, mine):
         pair_copy(i).wait_recv()
         for d in range(far, 0, -1):
             at = slice(d * band, (d + 1) * band)
             for c in range(2):
                 total = acc[i, c, at] + rp[i, c, at].astype(F32)
-                if i == own and d == far:
+                if mine and d == far:
                     dg[c] = total
                 else:
                     cb[i, d - 1, c] = total.astype(BF16)
-        x_send_part(i, 0)
-        if i in routed:
+        if not mine and routed(i):
             for h in range(parts):
                 d_copy(i, h).start()
+        elif not mine:
+            x_copy(i, 0, far).start()
+        for d in range(far - 1, 0, -1):
+            x_copy(i, 0, d).start()
         for c in range(2):
             zf[i, c] = acc[i, c, 0:band] + rp[i, c, 0:band].astype(F32)
 
     def send_far(h):
-        for i in routed:
+        for i in range(0, own, 2):
             d_copy(i, h).wait()
         for c in range(2):
             total = dg[c, part(h)]
-            for k in range(len(routed)):
+            for k in range(slabs // 2):
                 total += zd[k, c, part(h)].astype(F32)
             cb[own, far - 1, c, part(h)] = total.astype(BF16)
         x_copy(own, h, far).start()
 
     loads[1].wait()
-    compute_other(0)
-    pl.semaphore_wait(barrier, chips + slabs - 1)
-    pair_copy(0).start()
-    compute_own(0)
     for i in range(slabs):
-        if i + 1 < slabs:
-            compute_other(i + 1)
-            pair_copy(i + 1).start()
-        pair_band(i)
-        if i + 1 < slabs:
-            compute_own(i + 1)
-    if parts == 2:
-        for i in range(own - 1):
-            x_send_part(i, 1)
+        pb[i] = partial_sum(i, 1).astype(BF16)
+        if i == 0:
+            pl.semaphore_wait(barrier, chips + slabs - 1)
+        pair_copy(i).start()
+        if i > 0:
+            pair_band(i - 1, False)
+        acc[i] = partial_sum(i, 0)
+    pair_band(own, True)
+    for i in range(own - 1):
+        x_send_part(i, 1)
 
     rows = sums.shape[1] // 3
     count = cell_ref.shape[1]
-    chunk = min(count, 4096)
+    chunk = min(count, GRID)
     for copy in loads[2:]:
         copy.wait()
     sums[...] = jnp.zeros_like(sums)
@@ -361,7 +360,7 @@
             c1, s1 = turn[0, pl.ds(g, 1)], turn[1, pl.ds(g, 1)]
             sin = (s1 * c2 + c1 * s2).astype(BF16)
             at = pl.ds(pl.multiple_of(g * 16, 16), 16)
-            into = last_table if isinstance(t, int) else table.at[e, h]
+            into = table.at[e, h]
             into[at, 0:span] = sin
             into[at, span:2 * span] = (c1 * c2 - s1 * s2).astype(BF16)
             into[at, 2 * span:3 * span] = -sin
@@ -371,9 +370,6 @@
         return carry
 
     chunks = count // chunk
-
-    def grid(i):
-        lax.fori_loop((i * chunks) // slabs, ((i + 1) * chunks) // slabs, grid_step, 0)
 
     def z_copy(i, h):
         return remote(
@@ -436,100 +432,85 @@
             across_copy(e, h, d).wait_recv()
             spread_copy(e, h, d).start()
 
-    tile = min(local, 1024)
+    tile = min(local, TILE)
 
     def gathered(e, h):
         for d in range(chips):
             spread_copy(e, h, d).wait_recv()
 
-    def update_pass(e, h, begin=False):
+    order = [k ^ (k >> 1) for k in range(slabs)]
+    last = order[-1]
+    units = slabs * parts
+
+    def looped(count, work, before, after):
+        def step(k, carry):
+            for at, events in before.items():
+                @pl.when(k == at)
+                def _():
+                    for event in events:
+                        event()
+            work(k)
+            for at, events in after.items():
+                @pl.when(k == at)
+                def _():
+                    for event in events:
+                        event()
+            return carry
+
+        lax.fori_loop(0, count, step, 0)
+
+    def update_pass(k):
+        j, h = k % slabs, k // slabs
+        e = j ^ lax.shift_right_logical(j, 1)
         gathered(e, h)
 
         def step(i, carry):
             at = pl.ds(pl.multiple_of(i * tile, tile), tile)
             data = full[e, h].reshape(2 * span, width)
-            imag = dot(table[e, h, at, 0:2 * span], data)
-            real = dot(table[e, h, at, span:3 * span], data)
-            if not begin:
-                real += update_ref[0, at]
-                imag += update_ref[1, at]
-            update_ref[0, at] = real
-            update_ref[1, at] = imag
+            update_ref[1, at] += dot(table[e, h, at, 0:2 * span], data)
+            update_ref[0, at] += dot(table[e, h, at, span:3 * span], data)
             return carry
 
         lax.fori_loop(0, local // tile, step, 0)
 
-    def tables(begin, end):
-        final = last * parts + parts - 1
-        if begin <= final < end:
-            lax.fori_loop(begin, final, table_band, 0)
-            table_band(final, 0)
-            begin = final + 1
-        if begin < end:
-            lax.fori_loop(begin, end, table_band, 0)
-
-    order = [0] + sorted(range(1, slabs), key=lambda e: (e != 1, -e))
-    last = order[-1]
-    units = slabs * parts
-    final = parts - 1
+    def call(f, *args):
+        return functools.partial(f, *args)
 
     reduce_part(0, 0)
-    grid(0)
+    after = {}
     for i in range(1, own):
-        reduce_part(i, 0)
+        after.setdefault(min(chunks - 1, i + GRID_LATE), []).append(call(reduce_part, i, 0))
         if i == 1:
-            send_far(0)
-            if parts == 2:
-                x_send_part(own - 1, 1)
-                x_send_part(own, 1)
-        grid(i)
-    if parts == 2:
-        send_far(1)
-        reduce_part(0, 1)
-    grid(own)
+            after[min(chunks - 1, i + GRID_LATE)] += [
+                call(send_far, 0), call(x_send_part, own - 1, 1), call(x_send_part, own, 1)
+            ]
+    after.setdefault(max(chunks - 2, 0), []).extend([call(send_far, 1), call(reduce_part, 0, 1)])
+    looped(chunks, lambda k: grid_step(k, 0), {}, after)
     flat[...] = sums[...].T
-    if parts == 2:
-        for i in range(1, own - 1):
-            reduce_part(i, 1)
+    update_ref[...] = jnp.zeros_like(update_ref)
+    for i in range(1, own - 1):
+        reduce_part(i, 1)
     reduce_part(own, 0)
     residual_part(0)
     hand_on(0, 0)
-    if parts == 2:
-        reduce_part(own - 1, 1)
-        tables(0, 2)
-        reduce_part(own, 1)
-        tables(2, 3)
-        hand_on(1, 0)
-        residual_part(1)
-        hand_on(0, 1)
-        for e in order[2:-1]:
-            hand_on(e, 0)
-        relay(0, 0)
-        tables(3, 5)
-        hand_on(last, 0)
-        tables(5, units)
-        hand_on(1, 1)
-        relay(1, 0)
-        update_pass(0, 0, True)
-        for k, e in enumerate(order[2:]):
-            hand_on(e, 1)
-            if e != last:
-                relay(e, 0)
-                update_pass(order[k + 1], 0)
-        relay(last, 0)
-        relay(0, 1)
-        for e in order[2:]:
-            update_pass(e, 0)
-    else:
-        tables(0, units)
-        for e in order[1:]:
-            hand_on(e, 0)
-        relay(0, 0)
+    reduce_part(own - 1, 1)
+    middle = [call(hand_on, 1, 0), call(residual_part, 1), call(hand_on, 0, 1)]
+    middle += [call(hand_on, e, 0) for e in order[2:-1]] + [call(relay, 0, 0)]
+    looped(
+        units, lambda t: table_band(t, 0), {},
+        {1: [call(reduce_part, own, 1)], 2: middle, 4: [call(hand_on, last, 0)]},
+    )
+    hand_on(1, 1)
+    relay(1, 0)
+    before = {}
+    for k, e in enumerate(order[2:]):
+        before[k + 1] = [call(hand_on, e, 1), call(relay, e, 0)]
+    before[slabs - 2] += [call(relay, 0, 1)]
     for k, e in enumerate(order[1:]):
-        relay(e, final)
-        update_pass(order[k], final, parts == 1 and k == 0)
-    gathered(last, final)
-    last_ref[...] = full[last, final]
+        before[slabs + k] = [call(relay, e, 1)]
+    looped(units - 1, update_pass, before, {})
+    gathered(last, parts - 1)
+    last_ref[...] = full[last, parts - 1]
     for i in range(slabs):
         pair_copy(i).wait_send()
     for e in range(slabs):
@@ -545,26 +526,29 @@
 def finish_kernel(back, piece_ref, part_ref, last_ref, table_ref, residual_ref, update_ref, buffer, sent):
     dot = functools.partial(jnp.dot, preferred_element_type=F32)
     _, local, width = part_ref.shape
-    span = table_ref.shape[1] // 3
+    slabs, parts, _, span = table_ref.shape
+    span //= 3
+    last = (slabs - 1) ^ ((slabs - 1) >> 1)
     tiles, _, tile, _ = buffer.shape
     out = pltpu.make_async_copy(piece_ref, residual_ref, sent.at[tiles])
     out.start()
 
     def put(i):
-        at = pl.ds(pl.multiple_of(i * tile, tile), tile)
+        at = pl.ds(i * tile, tile)
         return pltpu.make_async_copy(buffer.at[i], update_ref.at[:, at], sent.at[i])
 
     def step(i, carry):
-        at = pl.ds(pl.multiple_of(i * tile, tile), tile)
+        at = pl.ds(i * tile, tile)
         data = last_ref[...].reshape(2 * span, width)
-        imag = dot(table_ref[at, 0:2 * span], data)
-        real = dot(table_ref[at, span:3 * span], data)
+        imag = dot(table_ref[last, parts - 1, at, 0:2 * span], data)
+        real = dot(table_ref[last, parts - 1, at, span:3 * span], data)
         buffer[i, 0] = (real + part_ref[0, at]) * back
         buffer[i, 1] = (imag + part_ref[1, at]) * back
         put(i).start()
         return carry
 
-    lax.fori_loop(0, tiles, step, 0)
+    for i in range(tiles):
+        step(i, 0)
     for i in range(tiles):
         put(i).wait()
     out.wait()
@@ -577,7 +561,7 @@
     rows = -(-band // 16) * 16
     vmem = pl.BlockSpec(memory_space=pltpu.VMEM)
     dma = pltpu.SemaphoreType.DMA
-    parts = 2 if band % 32 == 0 else 1
+    parts = 2
     share = band // parts
     span = facets * share
     piece, part, last, last_table = pl.pallas_call(
@@ -588,7 +572,7 @@
             jax.ShapeDtypeStruct((2, band, width), F32),
             jax.ShapeDtypeStruct((2, local, width), F32),
             jax.ShapeDtypeStruct((2, facets, share, width), BF16),
-            jax.ShapeDtypeStruct((local, 3 * span), BF16),
+            jax.ShapeDtypeStruct((slabs, parts, local, 3 * span), BF16),
         ],
         scratch_shapes=[
             pltpu.SMEM(subs.shape, jnp.int32),
@@ -611,7 +595,6 @@
             pltpu.VMEM((width, 3 * rows), F32),
             pltpu.VMEM((3 * rows, width), F32),
             pltpu.VMEM((slabs, parts, 2, facets, share, width), BF16),
-            pltpu.VMEM((slabs, parts, local, 3 * span), BF16),
             pltpu.VMEM((2, local // 16, span), F32),
             dma((5,)),
             dma((slabs,)), dma((slabs,)),
@@ -622,7 +605,7 @@
             dma((slabs, parts, chips - 1)), dma((slabs, parts, chips - 1)),
             dma((slabs, parts, chips)), dma((slabs, parts, chips)),
         ],
-        compiler_params=pltpu.CompilerParams(collective_id=0, has_side_effects=True, vmem_limit_bytes=40 * 1024 * 1024),
+        compiler_params=pltpu.CompilerParams(collective_id=0, has_side_effects=True, vmem_limit_bytes=36 * 1024 * 1024),
         name="fused",
     )(offset, *[pltpu.with_memory_space_constraint(x, pltpu.HBM) for x in (subs, slab, cells, values, weights)])
     tiles = local // min(local, 256)
@@ -651,7 +634,7 @@
     first = (facet_offset + lax.axis_index("slab") * local_rows).astype(jnp.int32)
     chips = facets // 2
     paired = facets == 2 * chips and chips == 4 and slabs > 2 and slabs & (slabs - 1) == 0
-    if owned == band and count_sub == facets and paired and band % 16 == 0 and local_rows % 256 == 0:
+    if owned == band and count_sub == facets and paired and band % 32 == 0 and local_rows % 256 == 0:
         residual, update = fused(
             facet_offset, subgrid_offset, slab[:, 0], vis_cell[0], vis_value[:, 0], vis_weight[0], slabs, facets
         )

time: 40.4 us -> 39.9 us (0.988)
  Pallas kernels: 38.9 us -> 38.4 us
where the time goes in v5:
time: 39.9 us; the launch traced here: 39.7 us
  Pallas kernels  38.4 us (96%)
  between operations  1.28 us (3%)
    pallas_call x1, Pallas kernels, fused(): pl.pallas_call(functools.partial(fused_kernel, 1.0 / math.sqrt(local * sl...  36.7 us
    pallas_call x1, Pallas kernels, fused(): pl.pallas_call(functools.partial(finish_kernel, 1.0 / math.sqrt(subs.shap...  1.66 us

profile of v5, /device:TPU:0, one launch (start us, length us, event | category | flops | bytes accessed | tf_op | source)
XLA Modules:
  0.0 39.7 jit_solution(1901774177186727134)
XLA Ops:
  1.3 36.7 %fused.1 = (f32[2,64,256]{2,1,0:T(8,128)S(1)}, f32[2,1024,256]{2,1,0:T(8,128)S(1)}, bf16[2,8,32,256]{3,2,1,0:T(8,128)(2,1)S(1)}, bf16[4,2,1024,768]{3,2,1,0:T(8,128)(2,1)S(1)}) custom-call(s32[1]{0:T(128)S(6)} %copy.10.offset_ref, s32[8]{0:T(128)} %subs_hbm.1, bf16[2,1024,256]{2,1,0:T(8,128)(2,1)} %bitcast.10, s32[1,32768]{1,0:T(1,128)} %bitcast.12, ...), custom_call_target="tpu_custom_call" | custom-call | tf_op jit(solution)/shard_map/fused/pallas_call | solution.py:567
  38.0 1.7 %finish.1 = (f32[2,64,256]{2,1,0:T(8,128)}, f32[2,1024,256]{2,1,0:T(8,128)}) custom-call(f32[2,64,256]{2,1,0:T(8,128)S(1)} %get-tuple-element.8.piece_ref, f32[2,1024,256]{2,1,0:T(8,128)S(1)} %get-tuple-element.9.part_ref, bf16[2,8,32,256]{3,2,1,0:T(8,128)(2,1)S(1)} %get-tuple-element.10.last_ref, bf16[4,2,1024,768]{3,2,1,0:T(8,128)(2,1)S(1)} %get-tuple-element.11.table_ref), custom_call_target="tpu_custom_call" | custom-call | tf_op jit(solution)/shard_map/finish/pallas_call | solution.py:612

commit v6 on v5

--- a/solution.py
+++ b/solution.py
@@ -234,10 +234,9 @@
         cos = jnp.concatenate(cos, axis=0)
         sin = jnp.concatenate(sin, axis=0)
         data = slab_ref[...].reshape(2 * local, width)
-        both = jnp.concatenate(
-            [jnp.concatenate([cos, sin], axis=1), jnp.concatenate([-sin, cos], axis=1)], axis=0
-        )
-        return dot(both, data).reshape(2, chips * band, width)
+        real = dot(jnp.concatenate([cos, sin], axis=1), data)
+        imag = dot(jnp.concatenate([-sin, cos], axis=1), data)
+        return real, imag
 
     def pair_copy(i):
         return remote(pb.at[i], rp.at[i], p_send.at[i], p_recv.at[i], facet=partner)
@@ -302,13 +301,15 @@
 
     loads[1].wait()
     for i in range(slabs):
-        pb[i] = partial_sum(i, 1).astype(BF16)
+        for c, half in enumerate(partial_sum(i, 1)):
+            pb[i, c] = half.astype(BF16)
         if i == 0:
             pl.semaphore_wait(barrier, chips + slabs - 1)
         pair_copy(i).start()
         if i > 0:
             pair_band(i - 1, False)
-        acc[i] = partial_sum(i, 0)
+        for c, half in enumerate(partial_sum(i, 0)):
+            acc[i, c] = half
     pair_band(own, True)
     for i in range(own - 1):
         x_send_part(i, 1)

time: 39.9 us -> 39.1 us (0.980)
  Pallas kernels: 38.4 us -> 37.6 us
    pallas_call x1, Pallas kernels: 36.7 us -> 36 us  [fused(): pl.pallas_call(functools.partial(fused_kernel, 1.0 / math.sqrt(local * sl...]
where the time goes in v6:
time: 39.1 us; the launch traced here: 38.9 us
  Pallas kernels  37.6 us (96%)
  between operations  1.28 us (3%)
    pallas_call x1, Pallas kernels, fused(): pl.pallas_call(functools.partial(fused_kernel, 1.0 / math.sqrt(local * sl...  36 us
    pallas_call x1, Pallas kernels, fused(): pl.pallas_call(functools.partial(finish_kernel, 1.0 / math.sqrt(subs.shap...  1.66 us

profile of v6, /device:TPU:0, one launch (start us, length us, event | category | flops | bytes accessed | tf_op | source)
XLA Modules:
  0.0 38.9 jit_solution(14956683316682118066)
XLA Ops:
  1.3 36.0 %fused.1 = (f32[2,64,256]{2,1,0:T(8,128)S(1)}, f32[2,1024,256]{2,1,0:T(8,128)S(1)}, bf16[2,8,32,256]{3,2,1,0:T(8,128)(2,1)S(1)}, bf16[4,2,1024,768]{3,2,1,0:T(8,128)(2,1)S(1)}) custom-call(s32[1]{0:T(128)S(6)} %copy.10.offset_ref, s32[8]{0:T(128)} %subs_hbm.1, bf16[2,1024,256]{2,1,0:T(8,128)(2,1)} %bitcast.10, s32[1,32768]{1,0:T(1,128)} %bitcast.12, ...), custom_call_target="tpu_custom_call" | custom-call | tf_op jit(solution)/shard_map/fused/pallas_call | solution.py:568
  37.2 1.7 %finish.1 = (f32[2,64,256]{2,1,0:T(8,128)}, f32[2,1024,256]{2,1,0:T(8,128)}) custom-call(f32[2,64,256]{2,1,0:T(8,128)S(1)} %get-tuple-element.8.piece_ref, f32[2,1024,256]{2,1,0:T(8,128)S(1)} %get-tuple-element.9.part_ref, bf16[2,8,32,256]{3,2,1,0:T(8,128)(2,1)S(1)} %get-tuple-element.10.last_ref, bf16[4,2,1024,768]{3,2,1,0:T(8,128)(2,1)S(1)} %get-tuple-element.11.table_ref), custom_call_target="tpu_custom_call" | custom-call | tf_op jit(solution)/shard_map/finish/pallas_call | solution.py:613

commit v7 on v6

--- a/solution.py
+++ b/solution.py
@@ -531,27 +531,29 @@
     span //= 3
     last = (slabs - 1) ^ ((slabs - 1) >> 1)
     tiles, _, tile, _ = buffer.shape
-    out = pltpu.make_async_copy(piece_ref, residual_ref, sent.at[tiles])
+    out = pltpu.make_async_copy(piece_ref, residual_ref, sent.at[2 * tiles])
     out.start()
 
-    def put(i):
+    def put(i, c):
         at = pl.ds(i * tile, tile)
-        return pltpu.make_async_copy(buffer.at[i], update_ref.at[:, at], sent.at[i])
+        return pltpu.make_async_copy(buffer.at[i, c], update_ref.at[c, at], sent.at[2 * i + c])
 
     def step(i, carry):
         at = pl.ds(i * tile, tile)
         data = last_ref[...].reshape(2 * span, width)
-        imag = dot(table_ref[last, parts - 1, at, 0:2 * span], data)
         real = dot(table_ref[last, parts - 1, at, span:3 * span], data)
         buffer[i, 0] = (real + part_ref[0, at]) * back
+        put(i, 0).start()
+        imag = dot(table_ref[last, parts - 1, at, 0:2 * span], data)
         buffer[i, 1] = (imag + part_ref[1, at]) * back
-        put(i).start()
+        put(i, 1).start()
         return carry
 
     for i in range(tiles):
         step(i, 0)
     for i in range(tiles):
-        put(i).wait()
+        for c in range(2):
+            put(i, c).wait()
     out.wait()
 
 
@@ -618,7 +620,7 @@
             jax.ShapeDtypeStruct((2, band, width), F32),
             jax.ShapeDtypeStruct((2, local, width), F32),
         ],
-        scratch_shapes=[pltpu.VMEM((tiles, 2, local // tiles, width), F32), dma((tiles + 1,))],
+        scratch_shapes=[pltpu.VMEM((tiles, 2, local // tiles, width), F32), dma((2 * tiles + 1,))],
         compiler_params=pltpu.CompilerParams(vmem_limit_bytes=8 * 1024 * 1024),
         name="finish",
     )(piece, part, last, last_table)

time: 39.1 us -> 39.1 us (level)
  no operation moved by 1% of the time
where the time goes in v7:
time: 39.1 us; the launch traced here: 38.9 us
  Pallas kernels  37.6 us (96%)
  between operations  1.28 us (3%)
    pallas_call x1, Pallas kernels, fused(): pl.pallas_call(functools.partial(fused_kernel, 1.0 / math.sqrt(local * sl...  36 us
    pallas_call x1, Pallas kernels, fused(): pl.pallas_call(functools.partial(finish_kernel, 1.0 / math.sqrt(subs.shap...  1.69 us

profile of v7, /device:TPU:0, one launch (start us, length us, event | category | flops | bytes accessed | tf_op | source)
XLA Modules:
  0.0 38.9 jit_solution(15131097786533393899)
XLA Ops:
  1.3 36.0 %fused.1 = (f32[2,64,256]{2,1,0:T(8,128)S(1)}, f32[2,1024,256]{2,1,0:T(8,128)S(1)}, bf16[2,8,32,256]{3,2,1,0:T(8,128)(2,1)S(1)}, bf16[4,2,1024,768]{3,2,1,0:T(8,128)(2,1)S(1)}) custom-call(s32[1]{0:T(128)S(6)} %copy.10.offset_ref, s32[8]{0:T(128)} %subs_hbm.1, bf16[2,1024,256]{2,1,0:T(8,128)(2,1)} %bitcast.10, s32[1,32768]{1,0:T(1,128)} %bitcast.12, ...), custom_call_target="tpu_custom_call" | custom-call | tf_op jit(solution)/shard_map/fused/pallas_call | solution.py:570
  37.2 1.7 %finish.1 = (f32[2,64,256]{2,1,0:T(8,128)}, f32[2,1024,256]{2,1,0:T(8,128)}) custom-call(f32[2,64,256]{2,1,0:T(8,128)S(1)} %get-tuple-element.8.piece_ref, f32[2,1024,256]{2,1,0:T(8,128)S(1)} %get-tuple-element.9.part_ref, bf16[2,8,32,256]{3,2,1,0:T(8,128)(2,1)S(1)} %get-tuple-element.10.last_ref, bf16[4,2,1024,768]{3,2,1,0:T(8,128)(2,1)S(1)} %get-tuple-element.11.table_ref), custom_call_target="tpu_custom_call" | custom-call | tf_op jit(solution)/shard_map/finish/pallas_call | solution.py:615
